TPU v7x, 128 devices: a whole 4x4x4 slice. The times are simulated.
128 devices in a mesh: vocab: 8 (over z, y_lo), rows: 16 (over y_hi, x, core).
Axes of the slice: x: 4, y: 4 (y_hi: 2, y_lo: 2; y = y_hi * 2 + y_lo), z: 4, core: 2. Of those that a mesh axis runs over, the one named last changes fastest.
Arguments:
- hidden_pass: bfloat16 [192, 64, 4096], P('rows', None, 'vocab'), may hold values from -6 to 6
- hidden_query: bfloat16 [192, 8, 4096], P('rows', None, 'vocab'), may hold values from -6 to 6
- mask_pass: int32 [192, 64], P('rows'), may hold values 0 or 1
- mask_query: int32 [192, 8], P('rows'), may hold values 0 or 1
- labels: int32 [192], P('rows'), may hold values from 0 to 191, each once
- head_weight: bfloat16 [4096, 16384], P('rows', 'vocab'), may hold values from -1 to 1
Outputs:
- grad_pass: bfloat16 [192, 64, 4096], P('rows', None, 'vocab')
- grad_query: bfloat16 [192, 8, 4096], P('rows', None, 'vocab')
Inputs may be any that keep to these rules, and one draw needn't show every extreme that they name: `labels`: each passage is the positive of exactly one query.
All inputs are finite; a program needn't handle non-finite values. No bound on the sum of `mask_pass` or of `mask_query` on one device may be relied on, other than what follows from the above.
Results may differ from a plain program's by a relative error of at most 0.018.
The roundings to bfloat16 on the way count: a program that leaves them out, or rounds other values in their place, can miss the bound.
Values may be sent and summed in bfloat16 or wider, within the bound.
A program may use at most 128 MiB of HBM per device.

v0:
```python
import jax
import jax.numpy as jnp
from jax import lax
from jax.sharding import PartitionSpec as P

V = 16384


MARGIN = 1.0
SHARPNESS = 16.0


def activate(logits):
    return jnp.log1p(jnp.maximum(logits, 0.0))


def pool_rows(logits, mask, groups, length):
    values = activate(logits).reshape(groups, length, -1)
    weight = mask.astype(jnp.float32)[:, :, None]
    totals = jnp.sum(values**4 * weight, axis=1)
    sparse = (jnp.power(totals + 1.0, 0.25) - 1.0).astype(jnp.bfloat16)
    return (values, totals, sparse)


def logit_slopes(sparse_grad, values, totals, logits, mask, groups, length):
    weight = mask.astype(jnp.float32)[:, :, None]
    factor = sparse_grad * jnp.power(totals + 1.0, -0.75)
    slopes = 1.0 / (1.0 + jnp.maximum(logits, 0.0)).reshape(groups, length, -1)
    gradient = factor[:, None, :] * weight * values**3 * slopes
    return gradient.astype(jnp.bfloat16).reshape(groups * length, -1)


def shards(hidden_pass, hidden_query, mask_pass, mask_query, labels, head_weight):
    groups = hidden_pass.shape[0]
    pass_length = hidden_pass.shape[1]
    query_length = hidden_query.shape[1]
    pass_rows = groups * pass_length
    whole_pass, whole_query = (
        lax.all_gather(hidden_pass, "vocab", axis=2, tiled=True),
        lax.all_gather(hidden_query, "vocab", axis=2, tiled=True),
    )
    tokens = jnp.concatenate(
        [whole_pass.reshape(pass_rows, -1), whole_query.reshape(groups * query_length, -1)], axis=0
    )
    whole_head = lax.all_gather(head_weight, "rows", axis=0, tiled=True)
    logits = jnp.dot(tokens, whole_head, preferred_element_type=jnp.float32)
    logits_pass = logits[:pass_rows]
    logits_query = logits[pass_rows:]
    values_pass, totals_pass, sparse_pass = pool_rows(logits_pass, mask_pass, groups, pass_length)
    values_query, totals_query, sparse_query = pool_rows(
        logits_query, mask_query, groups, query_length
    )
    all_pass = lax.all_gather(sparse_pass, "rows", axis=0, tiled=True)
    partial_scores = lax.dot_general(
        sparse_query, all_pass, (((1,), (1,)), ((), ())), preferred_element_type=jnp.float32
    )
    scaling = SHARPNESS * V ** (-0.5)
    scores = lax.psum(partial_scores, "vocab") * scaling
    onehot = (labels[:, None] == jnp.arange(all_pass.shape[0], dtype=jnp.int32)[None, :]).astype(
        jnp.float32
    )
    positive = jnp.sum(scores * onehot, axis=1, keepdims=True)
    weights = jax.nn.sigmoid(MARGIN + scores - positive) * (1.0 - onehot)
    score_grad = ((weights - onehot * jnp.sum(weights, axis=1, keepdims=True)) * scaling).astype(
        jnp.bfloat16
    )
    query_sparse_grad = jnp.dot(score_grad, all_pass, preferred_element_type=jnp.float32)
    pass_sparse_grad = lax.psum_scatter(
        lax.dot_general(
            score_grad, sparse_query, (((0,), (0,)), ((), ())), preferred_element_type=jnp.float32
        ).astype(jnp.bfloat16),
        "rows",
        scatter_dimension=0,
        tiled=True,
    ).astype(jnp.float32)
    slopes_pass = logit_slopes(
        pass_sparse_grad, values_pass, totals_pass, logits_pass, mask_pass, groups, pass_length
    )
    slopes_query = logit_slopes(
        query_sparse_grad,
        values_query,
        totals_query,
        logits_query,
        mask_query,
        groups,
        query_length,
    )
    slopes = jnp.concatenate([slopes_pass, slopes_query], axis=0)
    partial_terms = lax.dot_general(
        slopes, whole_head, (((1,), (1,)), ((), ())), preferred_element_type=jnp.float32
    )
    summed = lax.psum_scatter(
        partial_terms.astype(jnp.bfloat16), "vocab", scatter_dimension=1, tiled=True
    ).astype(jnp.float32)
    grad_pass = summed[:pass_rows].reshape(groups, pass_length, -1).astype(jnp.bfloat16)
    grad_query = summed[pass_rows:].reshape(groups, query_length, -1).astype(jnp.bfloat16)
    return (grad_pass, grad_query)


def solution(mesh):
    return jax.shard_map(
        shards,
        mesh=mesh,
        in_specs=(
            P("rows", None, "vocab"),
            P("rows", None, "vocab"),
            P("rows", None),
            P("rows", None),
            P("rows"),
            P("rows", "vocab"),
        ),
        out_specs=(P("rows", None, "vocab"), P("rows", None, "vocab")),
        check_vma=False,
    )
```

profile of v0, /device:TPU:1, one launch (start us, length us, event | category | flops | bytes accessed | tf_op | source)
XLA Modules:
  0.0 582.5 jit_solution(7997053838802702710)
XLA Ops:
  7.2 0.7 all-gather.4.cloned.1.call-update
  7.9 0.7 all-gather.6.cloned.1.call-update
  8.7 0.7 convert_element_type.48
  9.4 0.7 convert_element_type.46
  10.3 1.2 dynamic-slice.4
  12.2 35.3 %all_gather.13 = bf16[12,8,4096]{2,1,0:T(8,128)(2,1)S(1)} all-gather(bf16[12,8,512]{2,1,0:T(8,128)(2,1)} %param.7), channel_id=1, replica_groups=mesh['vocab'=8,'rows'=16] {'vocab'}, dimensions={2}, use_global_device_ids=true | all-gather | bytes 884736 | tf_op jit(solution)/shard_map/all_gather | solution.py:40
  47.5 106.5 %all-gather.4.cloned.1.call-done = bf16[12,64,4096]{2,1,0:T(8,128)(2,1)} async-done(((bf16[12,64,512]{2,1,0:T(8,128)(2,1)}), bf16[12,64,4096]{2,1,0:T(8,128)(2,1)}) %all-gather.4.cloned.1.call-update) | async-done | bytes 6291472 | tf_op jit(solution)/shard_map/all_gather | solution.py:39
  154.0 113.4 %all-gather.6.cloned.1.call-done = bf16[4096,2048]{1,0:T(8,128)(2,1)} async-done(((bf16[256,2048]{1,0:T(8,128)(2,1)}), bf16[4096,2048]{1,0:T(8,128)(2,1)}) %all-gather.6.cloned.1.call-update) | async-done | bytes 16777232 | tf_op jit(solution)/shard_map/all_gather | solution.py:45
  267.4 18.5 %fusion.1 = f32[864,2048]{1,0:T(8,128)S(1)} fusion(bf16[4096,2048]{1,0:T(8,128)(2,1)} %all-gather.6.cloned.1.call-done, bf16[96,4096]{1,0:T(8,128)(2,1)S(1)} %bitcast.31, bf16[768,4096]{1,0:T(8,128)(2,1)} %bitcast.32), kind=kOutput, calls=%fused_computation.2 | convolution fusion | flops 14509670400 | bytes 30932992 | tf_op jit(solution)/shard_map/dot_general | solution.py:46
  285.9 2.4 multiply_multiply_fusion.1
  288.3 0.5 copy-done
  288.8 0.5 fusion.13
  289.3 1.1 multiply_reduce_fusion
  290.5 22.7 %all-gather = bf16[16,12,2048]{2,1,0:T(8,128)(2,1)S(1)} all-gather(bf16[1,12,2048]{2,1,0:T(8,128)(2,1)S(1)} %fusion.17), channel_id=1, replica_groups=mesh['vocab'=8,'rows'=16] {'rows'}, dimensions={0}, use_global_device_ids=true | all-gather | bytes 835584 | tf_op jit(solution)/shard_map/all_gather | solution.py:53
  313.3 0.3 fusion.18
  313.7 27.5 %psum.7 = f32[12,192]{1,0:T(8,128)S(1)} all-reduce(f32[12,192]{1,0:T(8,128)S(1)} %fusion.18), channel_id=1, replica_groups=mesh['vocab'=8,'rows'=16] {'vocab'}, use_global_device_ids=true, to_apply=%region_2.0 | all-reduce | flops 2304 | bytes 18432 | tf_op jit(solution)/shard_map/psum | solution.py:58
  341.1 0.2 select_reduce_fusion
  341.3 0.2 fusion.27
  341.5 0.5 convolution_convert_fusion.1
  342.0 45.0 %fusion = bf16[16,2048]{1,0:T(8,128)(2,1)S(1)} fusion(bf16[192,2048]{1,0:T(8,128)(2,1)S(1)} %convolution_convert_fusion.1), kind=kCustom, calls=%all-reduce-scatter | all-reduce-scatter fusion | flops 524289 | bytes 852480
  387.1 1.9 collective-permute-start
  389.0 1.3 collective-permute-start.1
  390.3 4.3 collective-permute-start.2
  394.6 0.3 convolution_multiply_fusion
  394.9 7.4 %collective-permute-start.3 = (bf16[12,2048]{1,0:T(8,128)(2,1)S(1)}, bf16[12,2048]{1,0:T(8,128)(2,1)S(1)}, u32[]{:S(2)}, u32[]{:S(2)}) collective-permute-start(bf16[12,2048]{1,0:T(8,128)(2,1)S(1)} %slice.22), channel_id=1, source_target_pairs={{0,4},{1,5},{2,6},{3,7},{4,8},{5,9},{6,10},{7,11},{8,12},{9,13},{1... | collective-permute-start | bytes 147464
  402.3 1.6 fusion.16
  403.9 0.7 concatenate.8
  404.7 5.3 fusion.7
  410.0 20.2 %convolution_convert_fusion = bf16[864,4096]{1,0:T(8,128)(2,1)} fusion(bf16[4096,2048]{1,0:T(8,128)(2,1)} %all-gather.6.cloned.1.call-done, bf16[96,2048]{1,0:T(8,128)(2,1)S(1)} %fusion.16, bf16[768,2048]{1,0:T(8,128)(2,1)S(1)} %fusion.7), kind=kOutput, calls=%fused_computation.6 | convolution fusion | flops 14506131456 | bytes 27394048 | tf_op jit(solution)/shard_map/dot_general | solution.py:89
  430.2 142.1 %reduce-scatter.4.cloned.1.call-done = bf16[864,512]{1,0:T(8,128)(2,1)} async-done(((bf16[864,4096]{1,0:T(8,128)(2,1)}), bf16[864,512]{1,0:T(8,128)(2,1)}) %reduce-scatter.4.cloned.1.call-update) | async-done | bytes 884752 | tf_op jit(solution)/shard_map/reduce_scatter | solution.py:92
  572.4 2.1 slice.20
  574.4 1.5 slice_bitcast_fusion
  (18 shorter events, 0.7 us)
Async XLA Ops:
  7.2 146.8 %all-gather.4.cloned.1.call-start = ((), (), s32[]{:S(2)}) async-start(), calls=%async_computation.1 | async-start | bytes 7077888 | tf_op jit(solution)/shard_map/all_gather | solution.py:39
  7.9 259.5 %all-gather.6.cloned.1.call-start = ((), (), s32[]{:S(2)}) async-start(), calls=%async_computation.2 | async-start | bytes 17825792 | tf_op jit(solution)/shard_map/all_gather | solution.py:45
  8.6 563.7 %reduce-scatter.4.cloned.1.call-start = ((), (), s32[]{:S(2)}) async-start(), calls=%async_computation.3 | async-start | bytes 7962624 | tf_op jit(solution)/shard_map/reduce_scatter | solution.py:92
  285.9 2.9 copy-start
  288.8 52.3 %copy-start.1 = (s32[12]{0:T(128)S(1)}, s32[12]{0:T(128)}, u32[]{:S(2)}) copy-start(s32[12]{0:T(128)} %param.10) | copy-start | bytes 148
  387.1 16.8 %collective-permute-start = (bf16[16,2048]{1,0:T(8,128)(2,1)S(1)}, bf16[16,2048]{1,0:T(8,128)(2,1)S(1)}, u32[]{:S(2)}, u32[]{:S(2)}) collective-permute-start(bf16[16,2048]{1,0:T(8,128)(2,1)S(1)} %fusion), channel_id=1, source_target_pairs={{0,1},{1,2},{2,3},{3,4},{4,5},{5,6},{6,7},{7,8},{8,9},{9,10},{10,1... | collective-permute-start | bytes 196616
  389.0 14.9 %collective-permute-start.1 = (bf16[16,2048]{1,0:T(8,128)(2,1)S(1)}, bf16[16,2048]{1,0:T(8,128)(2,1)S(1)}, u32[]{:S(2)}, u32[]{:S(2)}) collective-permute-start(bf16[16,2048]{1,0:T(8,128)(2,1)S(1)} %fusion), channel_id=1, source_target_pairs={{0,2},{1,3},{2,4},{3,5},{4,6},{5,7},{6,8},{7,9},{8,10},{9,11},{10,... | collective-permute-start | bytes 196616
  390.3 13.6 %collective-permute-start.2 = (bf16[16,2048]{1,0:T(8,128)(2,1)S(1)}, bf16[16,2048]{1,0:T(8,128)(2,1)S(1)}, u32[]{:S(2)}, u32[]{:S(2)}) collective-permute-start(bf16[16,2048]{1,0:T(8,128)(2,1)S(1)} %fusion), channel_id=1, source_target_pairs={{0,3},{1,4},{2,5},{3,6},{4,7},{5,8},{6,9},{7,10},{8,11},{9,12},{10... | collective-permute-start | bytes 196616
  394.9 9.0 %collective-permute-start.3 = (bf16[12,2048]{1,0:T(8,128)(2,1)S(1)}, bf16[12,2048]{1,0:T(8,128)(2,1)S(1)}, u32[]{:S(2)}, u32[]{:S(2)}) collective-permute-start(bf16[12,2048]{1,0:T(8,128)(2,1)S(1)} %slice.22), channel_id=1, source_target_pairs={{0,4},{1,5},{2,6},{3,7},{4,8},{5,9},{6,10},{7,11},{8,12},{9,13},{1... | collective-permute-start | bytes 147464
Sparse Core Ops, SparseCore 0:
  9.6 144.2 all-gather.3
  156.4 110.9 all-gather.5
  430.4 141.9 reduce-scatter.3
where the time goes:
time: 583 us
  waiting for transfers between devices  363 us (62%)
  blocking collectives  130 us (22%)
  matrix products  39.7 us (7%)
  starting transfers between devices  15 us (3%)
  between operations  14.6 us (3%)
  other arithmetic  12.8 us (2%)
  local copies, waits for them, and re-layouts  6.48 us (1%)
    reduce_scatter x1, waiting for transfers between devices, shards(): lax.psum_scatter(partial_terms.astype(jnp.bfloat16), 'vocab', scatter_dim...  142 us
    all_gather x1, waiting for transfers between devices, shards(): whole_head = lax.all_gather(head_weight, 'rows', axis=0, tiled=True)  113 us
    all_gather x1, waiting for transfers between devices, shards(): lax.all_gather(hidden_pass, 'vocab', axis=2, tiled=True)  106 us
    unnamed x1, blocking collectives  45 us
    all_gather x1, blocking collectives, shards(): lax.all_gather(hidden_query, 'vocab', axis=2, tiled=True)  35.3 us
    psum x1, blocking collectives, shards(): scores = lax.psum(partial_scores, 'vocab') * scaling  27.5 us
    all_gather x1, blocking collectives, shards(): all_pass = lax.all_gather(sparse_pass, 'rows', axis=0, tiled=True)  22.7 us
    dot_general x1, matrix products, shards(): lax.dot_general(slopes, whole_head, (((1,), (1,)), ((), ())), preferred_e...  20.2 us
  transfers between devices with their start and end apart: 7, of which 3 were waited for; matrix products, arithmetic and copies ran while one was open for 1% of the time, Pallas kernels for 0%

commit v1 on v0

v1 whole, which is shorter than its diff:
```python
import jax
import jax.numpy as jnp
from jax import lax
from jax.experimental import pallas as pl
from jax.experimental.pallas import tpu as pltpu
from jax.sharding import PartitionSpec as P

MESH = pl.DeviceIdType.MESH
MARGIN = 1.0
SHARPNESS = 16.0
V = 16384
SCALING = SHARPNESS * V ** (-0.5)

G = 12
LP = 64
LQ = 8
PR = G * LP
QR = G * LQ
R = PR + QR
RH = R // 2
F = 512
W = 2048
HD = 256
HH = HD // 2
PAD = 16
ROWS = 16
VOCAB = 8
BF = jnp.bfloat16
F32 = jnp.float32

RELATIVE = [(1, 0), (3, 0), (2, 0), (0, 1), (1, 1), (3, 1), (2, 1)]


def where_am_i():
    v = lax.axis_index("vocab")
    r = lax.axis_index("rows")
    return v // 2, v % 2, r // 8, (r // 2) % 4, r % 2


def device(z, yl, yh, x, c):
    return (z * 2 + yl, (yh * 4 + x) * 2 + c)


def kernel(
    hp_ref,
    hq_ref,
    mp_ref,
    mq_ref,
    lab_ref,
    hw_ref,
    gp_ref,
    gq_ref,
    tok,
    head,
    acc,
    slopes,
    totals,
    factor,
    allp,
    allq,
    sbuf,
    gbuf,
    rhalf,
    rfull,
    ybuf,
    lsem,
    ssem,
    rsem,
):
    z, yl, yh, x, c = where_am_i()
    v = z * 2 + yl
    r = (yh * 4 + x) * 2 + c
    zs = [z, (z + 1) % 4, (z + 2) % 4, (z + 3) % 4]
    xs = [x, (x + 1) % 4, (x + 2) % 4, (x + 3) % 4]
    yls = [yl, 1 - yl]
    yhs = [yh, 1 - yh]
    cs = [c, 1 - c]
    zdev = [device(k, yl, yh, x, c) for k in zs]
    xdev = [device(z, yl, yh, k, c) for k in xs]
    yldev = device(z, 1 - yl, yh, x, c)
    yhdev = device(z, yl, 1 - yh, x, c)
    cdev = device(z, yl, yh, x, 1 - c)

    own_head = yh * 4 + x
    local = [
        pltpu.make_async_copy(hp_ref, tok.at[v, pl.ds(0, PR)], lsem.at[0]),
        pltpu.make_async_copy(hq_ref, tok.at[v, pl.ds(PR, QR)], lsem.at[1]),
        pltpu.make_async_copy(hw_ref, head.at[own_head, pl.ds(c * HD, HD)], lsem.at[2]),
    ]
    for copy in local:
        copy.start()

    peers = [device(zs[d], yls[e], yh, x, c) for d, e in RELATIVE]
    peers += [device(z, yl, yhs[e], xs[d], c) for d, e in RELATIVE]
    peers += [device(z, yl, yhs[e], xs[d], 1 - c) for d, e in [(0, 0)] + RELATIVE]
    barrier = pltpu.get_barrier_semaphore()
    for peer in peers:
        pl.semaphore_signal(barrier, inc=1, device_id=peer, device_id_type=MESH)
    pl.semaphore_wait(barrier, len(peers))
    for copy in local:
        copy.wait()

    counter = [0]
    sent = []

    def remote(src, dst, dev):
        k = counter[0]
        counter[0] += 1
        copy = pltpu.make_async_remote_copy(
            src_ref=src,
            dst_ref=dst,
            send_sem=ssem.at[k],
            recv_sem=rsem.at[k],
            device_id=dev,
            device_id_type=MESH,
        )
        copy.start()
        return copy

    def send(ref, dev):
        copy = remote(ref, ref, dev)
        sent.append(copy)
        return copy

    def hid(dz, dy, h):
        return tok.at[zs[dz] * 2 + yls[dy], pl.ds(h * RH, RH)]

    def hed(dx, dy, h):
        return head.at[yhs[dy] * 4 + xs[dx], pl.ds(c * HD + h * HH, HH)]

    a, b, s = {}, {}, {}
    tok_sent = []

    def a_send(key, ref, dev):
        copy = remote(ref, ref, dev)
        a[key] = copy
        tok_sent.append(copy)

    def b_send(key, ref, dev):
        b[key] = send(ref, dev)

    def to_core(dx, dy, h):
        s[(dx, dy, h)] = send(hed(dx, dy, h), cdev)

    a_send(("y", 0), hid(0, 0, 0), yldev)
    b_send(("y", 0), hed(0, 0, 0), yhdev)
    a_send(("+", 0), hid(0, 0, 0), zdev[1])
    a_send(("-", 1), hid(0, 0, 1), zdev[3])
    b_send(("+", 0), hed(0, 0, 0), xdev[1])
    b_send(("-", 1), hed(0, 0, 1), xdev[3])
    a_send(("y", 1), hid(0, 0, 1), yldev)
    b_send(("y", 1), hed(0, 0, 1), yhdev)
    a_send(("+", 1), hid(0, 0, 1), zdev[1])
    a_send(("-", 0), hid(0, 0, 0), zdev[3])
    b_send(("+", 1), hed(0, 0, 1), xdev[1])
    b_send(("-", 0), hed(0, 0, 0), xdev[3])
    to_core(0, 0, 0)
    to_core(0, 0, 1)

    a[("+", 0)].wait_recv()
    a_send("f+", hid(3, 0, 0), zdev[1])
    a[("-", 1)].wait_recv()
    a_send("f-", hid(1, 0, 1), zdev[3])
    b[("+", 0)].wait_recv()
    b_send("f+", hed(3, 0, 0), xdev[1])
    b[("-", 1)].wait_recv()
    b_send("f-", hed(1, 0, 1), xdev[3])
    to_core(3, 0, 0)
    to_core(1, 0, 1)

    a[("y", 0)].wait_recv()
    a_send(("o+", 0), hid(0, 1, 0), zdev[1])
    a_send(("o-", 0), hid(0, 1, 0), zdev[3])
    b[("y", 0)].wait_recv()
    b_send(("o+", 0), hed(0, 1, 0), xdev[1])
    b_send(("o-", 0), hed(0, 1, 0), xdev[3])
    a[("y", 1)].wait_recv()
    a_send(("o-", 1), hid(0, 1, 1), zdev[3])
    a_send(("o+", 1), hid(0, 1, 1), zdev[1])
    b[("y", 1)].wait_recv()
    b_send(("o-", 1), hed(0, 1, 1), xdev[3])
    b_send(("o+", 1), hed(0, 1, 1), xdev[1])
    to_core(0, 1, 0)
    to_core(0, 1, 1)
    b[("+", 1)].wait_recv()
    to_core(3, 0, 1)
    b[("-", 0)].wait_recv()
    to_core(1, 0, 0)
    a[("o+", 0)].wait_recv()
    a_send("g+", hid(3, 1, 0), zdev[1])
    b[("o+", 0)].wait_recv()
    b_send("g+", hed(3, 1, 0), xdev[1])
    to_core(3, 1, 0)
    a[("o-", 1)].wait_recv()
    a_send("g-", hid(1, 1, 1), zdev[3])
    b[("o-", 1)].wait_recv()
    b_send("g-", hed(1, 1, 1), xdev[3])
    to_core(1, 1, 1)
    b["f+"].wait_recv()
    to_core(2, 0, 0)
    b["f-"].wait_recv()
    to_core(2, 0, 1)
    for key in [("+", 1), ("-", 0), "f+", "f-", ("o-", 0), ("o+", 1), "g+", "g-"]:
        a[key].wait_recv()

    def mm1(dx, dy, first):
        slot = yhs[dy] * 4 + xs[dx]
        for h in (0, 1):
            s[(dx, dy, h)].wait_recv()

        @pl.loop(0, W // 256)
        def _(n):
            cols = pl.ds(pl.multiple_of(n * 256, 256), 256)
            product = jnp.dot(tok[slot], head[slot, :, cols], preferred_element_type=F32)
            if first:
                acc[:, cols] = product
            else:
                acc[:, cols] += product

    mm1(0, 0, True)
    mm1(1, 0, False)
    mm1(3, 0, False)
    b[("o+", 1)].wait_recv()
    to_core(3, 1, 1)
    b[("o-", 0)].wait_recv()
    to_core(1, 1, 0)
    mm1(0, 1, False)
    mm1(2, 0, False)
    mm1(1, 1, False)
    mm1(3, 1, False)
    b["g+"].wait_recv()
    to_core(2, 1, 0)
    b["g-"].wait_recv()
    to_core(2, 1, 1)
    mm1(2, 1, False)

    totals[...] = jnp.zeros_like(totals)

    def pool(base, length, mask_ref, k, side):
        rows = pl.ds(pl.multiple_of(base + k * length, 8), length)
        line = mask_ref[pl.ds(k, 1), :].astype(F32)
        eye = lax.broadcasted_iota(jnp.int32, (length, length), 0) == lax.broadcasted_iota(
            jnp.int32, (length, length), 1
        )
        weight = jnp.sum(
            jnp.where(eye, jnp.broadcast_to(line, (length, length)), 0.0), axis=1, keepdims=True
        )
        for n in range(W // 256):
            cols = pl.ds(n * 256, 256)
            high = jnp.maximum(acc[rows, cols], 0.0)
            act = jnp.log1p(high)
            square = act * act
            totals[side, pl.ds(k, 1), cols] = jnp.sum(
                square * square * weight, axis=0, keepdims=True
            )
            acc[rows, cols] = weight * (square * act) / (1.0 + high)

    @pl.loop(0, G)
    def _(k):
        pool(0, LP, mp_ref, k, 0)
        pool(PR, LQ, mq_ref, k, 1)

    def fourth_root(t):
        return jnp.sqrt(jnp.sqrt(t))

    allp[r] = (fourth_root(totals[0] + 1.0) - 1.0).astype(BF)
    allq[r] = (fourth_root(totals[1] + 1.0) - 1.0).astype(BF)

    def spread(ref):
        copies = [send(ref.at[r], device(z, yl, yhs[e], xs[d], c)) for d, e in RELATIVE]
        copies.append(send(ref.at[r], cdev))
        return copies

    def hand_on(ref, copies):
        handed = []
        for (d, e), copy in zip(RELATIVE, copies):
            copy.wait_recv()
            came = (yhs[e] * 4 + xs[(4 - d) % 4]) * 2 + c
            handed.append(send(ref.at[came], cdev))
        return handed

    spread_p = spread(allp)
    spread_q = spread(allq)
    handed_p = hand_on(allp, spread_p)
    spread_p[7].wait_recv()
    for copy in handed_p:
        copy.wait_recv()

    every_pass = allp[...].reshape(ROWS * PAD, W)
    sbuf[v] = lax.dot_general(
        allq[r], every_pass, (((1,), (1,)), ((), ())), preferred_element_type=F32
    )
    shared = [send(sbuf.at[v], device(zs[d], yls[e], yh, x, c)) for d, e in RELATIVE]
    handed_q = hand_on(allq, spread_q)
    row_at = lax.broadcasted_iota(jnp.int32, (PAD, ROWS * PAD), 0)
    col_at = lax.broadcasted_iota(jnp.int32, (PAD, ROWS * PAD), 1)
    passage = (col_at // PAD) * G + col_at % PAD
    real = (col_at % PAD < G) & (row_at < G)
    label = jnp.full((PAD, ROWS * PAD), -1, jnp.int32)
    for q in range(G):
        label = jnp.where(row_at == q, lab_ref[q], label)
    chosen = (label == passage) & real
    for copy in shared:
        copy.wait_recv()
    scores = sbuf[0]
    for k in range(1, VOCAB):
        scores = scores + sbuf[k]
    scores = scores * SCALING
    onehot = jnp.where(chosen, 1.0, 0.0)
    positive = jnp.sum(scores * onehot, axis=1, keepdims=True)
    weights = jnp.where(
        real & jnp.logical_not(chosen), jax.nn.sigmoid(MARGIN + scores - positive), 0.0
    )
    score_grad = (
        (weights - onehot * jnp.sum(weights, axis=1, keepdims=True)) * SCALING
    ).astype(BF)
    gbuf[r] = score_grad
    group = [send(gbuf.at[r], device(z, yl, yhs[e], xs[d], cs[f])) for d, e in RELATIVE for f in (0, 1)]
    group.append(send(gbuf.at[r], cdev))

    def tail(t):
        root = jnp.sqrt(t)
        return 1.0 / (root * jnp.sqrt(root))

    query_grad = jnp.dot(score_grad, every_pass, preferred_element_type=F32)
    factor[1] = query_grad * tail(totals[1] + 1.0)

    @pl.loop(0, G // 2)
    def _(k):
        rows = pl.ds(pl.multiple_of(PR + k * 2 * LQ, 2 * LQ), 2 * LQ)
        upper = lax.broadcasted_iota(jnp.int32, (2 * LQ, W), 0) < LQ
        gain = jnp.where(
            upper,
            jnp.broadcast_to(factor[1, pl.ds(2 * k, 1), :], (2 * LQ, W)),
            jnp.broadcast_to(factor[1, pl.ds(2 * k + 1, 1), :], (2 * LQ, W)),
        )
        slopes[rows, :] = (acc[rows, :] * gain).astype(BF)

    spread_q[7].wait_recv()
    for copy in handed_q:
        copy.wait_recv()
    for copy in group:
        copy.wait_recv()
    pick = jnp.where(
        lax.broadcasted_iota(jnp.int32, (ROWS * PAD, PAD), 0)
        == r * PAD + lax.broadcasted_iota(jnp.int32, (ROWS * PAD, PAD), 1),
        1.0,
        0.0,
    ).astype(BF)
    mine = jnp.dot(
        gbuf[...].reshape(ROWS * PAD, ROWS * PAD), pick, preferred_element_type=F32
    ).astype(BF)
    pass_grad = lax.dot_general(
        mine,
        allq[...].reshape(ROWS * PAD, W),
        (((0,), (0,)), ((), ())),
        preferred_element_type=F32,
    )
    factor[0] = pass_grad * tail(totals[0] + 1.0)

    @pl.loop(0, G)
    def _(k):
        rows = pl.ds(pl.multiple_of(k * LP, LP), LP)
        slopes[rows, :] = (acc[rows, :] * factor[0, pl.ds(k, 1), :]).astype(BF)

    for copy in tok_sent:
        copy.wait_send()

    def mm2(dz, dy):
        slot = zs[dz] * 2 + yls[dy]

        @pl.loop(0, F // 256)
        def _(n):
            cols = pl.ds(pl.multiple_of(n * 256, 256), 256)
            tok[slot, :, cols] = lax.dot_general(
                slopes[...],
                head[slot, cols, :],
                (((1,), (1,)), ((), ())),
                preferred_element_type=F32,
            ).astype(BF)

    def add_into(slot, h, other):
        @pl.loop(0, RH // 48)
        def _(k):
            rows = pl.ds(pl.multiple_of(h * RH + k * 48, 16), 48)
            some = pl.ds(pl.multiple_of(k * 48, 16), 48)
            tok[slot, rows, :] = (
                tok[slot, rows, :].astype(F32) + other[some, :].astype(F32)
            ).astype(BF)

    def out(src, dst, dev):
        copy = remote(src, dst, dev)
        sent.append(copy)
        return copy

    arrivals = {}
    for dy in (1, 0):
        mm2(2, dy)
        up = out(hid(2, dy, 0), rhalf.at[dy, 0], zdev[1])
        down = out(hid(2, dy, 1), rhalf.at[dy, 1], zdev[3])
        mm2(1, dy)
        arrivals[(dy, 0, 1)] = out(hid(1, dy, 1), rfull.at[dy, 0, pl.ds(RH, RH)], zdev[1])
        mm2(3, dy)
        arrivals[(dy, 1, 0)] = out(hid(3, dy, 0), rfull.at[dy, 1, pl.ds(0, RH)], zdev[3])
        up.wait_recv()
        add_into(zs[1] * 2 + yls[dy], 0, rhalf.at[dy, 0])
        arrivals[(dy, 0, 0)] = out(hid(1, dy, 0), rfull.at[dy, 0, pl.ds(0, RH)], zdev[1])
        down.wait_recv()
        add_into(zs[3] * 2 + yls[dy], 1, rhalf.at[dy, 1])
        arrivals[(dy, 1, 1)] = out(hid(3, dy, 1), rfull.at[dy, 1, pl.ds(RH, RH)], zdev[3])
    mm2(0, 1)
    mm2(0, 0)

    slot = z * 2 + (1 - yl)
    across = []
    for h in (0, 1):
        arrivals[(1, 0, h)].wait_recv()
        arrivals[(1, 1, h)].wait_recv()

        @pl.loop(0, RH // 48)
        def _(k):
            rows = pl.ds(pl.multiple_of(h * RH + k * 48, 16), 48)
            tok[slot, rows, :] = (
                tok[slot, rows, :].astype(F32)
                + rfull[1, 0, rows, :].astype(F32)
                + rfull[1, 1, rows, :].astype(F32)
            ).astype(BF)

        across.append(out(hid(0, 1, h), ybuf.at[pl.ds(h * RH, RH)], yldev))
    for copy in across:
        copy.wait_recv()
    for key in [(0, 0, 0), (0, 0, 1), (0, 1, 0), (0, 1, 1)]:
        arrivals[key].wait_recv()

    def total(rows):
        return (
            tok[v, rows, :].astype(F32)
            + rfull[0, 0, rows, :].astype(F32)
            + rfull[0, 1, rows, :].astype(F32)
            + ybuf[rows, :].astype(F32)
        ).astype(BF)

    @pl.loop(0, PR // 48)
    def _(k):
        rows = pl.ds(pl.multiple_of(k * 48, 16), 48)
        gp_ref[rows, :] = total(rows)

    for k in range(QR // 48):
        gq_ref[pl.ds(k * 48, 48), :] = total(pl.ds(PR + k * 48, 48))

    for copy in sent:
        copy.wait_send()


COPIES = 150


def shards(hidden_pass, hidden_query, mask_pass, mask_query, labels, head_weight):
    anywhere = pl.BlockSpec(memory_space=pl.ANY)
    vmem = pl.BlockSpec(memory_space=pltpu.VMEM)
    smem = pl.BlockSpec(memory_space=pltpu.SMEM)
    grad_pass, grad_query = pl.pallas_call(
        kernel,
        out_shape=(
            jax.ShapeDtypeStruct((PR, F), BF),
            jax.ShapeDtypeStruct((QR, F), BF),
        ),
        in_specs=[anywhere, anywhere, vmem, vmem, smem, anywhere],
        out_specs=(vmem, vmem),
        scratch_shapes=[
            pltpu.VMEM((VOCAB, R, F), BF),
            pltpu.VMEM((VOCAB, 2 * HD, W), BF),
            pltpu.VMEM((R, W), F32),
            pltpu.VMEM((R, W), BF),
            pltpu.VMEM((2, PAD, W), F32),
            pltpu.VMEM((2, PAD, W), F32),
            pltpu.VMEM((ROWS, PAD, W), BF),
            pltpu.VMEM((ROWS, PAD, W), BF),
            pltpu.VMEM((VOCAB, PAD, ROWS * PAD), F32),
            pltpu.VMEM((ROWS, PAD, ROWS * PAD), BF),
            pltpu.VMEM((2, 2, RH, F), BF),
            pltpu.VMEM((2, 2, R, F), BF),
            pltpu.VMEM((R, F), BF),
            pltpu.SemaphoreType.DMA((3,)),
            pltpu.SemaphoreType.DMA((COPIES,)),
            pltpu.SemaphoreType.DMA((COPIES,)),
        ],
        compiler_params=pltpu.CompilerParams(
            collective_id=0, has_side_effects=True, vmem_limit_bytes=60 * 1024 * 1024
        ),
        name="step",
    )(
        hidden_pass.reshape(PR, F),
        hidden_query.reshape(QR, F),
        mask_pass,
        mask_query,
        labels,
        head_weight,
    )
    return (
        grad_pass.reshape(G, LP, F),
        grad_query.reshape(G, LQ, F),
    )


def solution(mesh):
    return jax.shard_map(
        shards,
        mesh=mesh,
        in_specs=(
            P("rows", None, "vocab"),
            P("rows", None, "vocab"),
            P("rows", None),
            P("rows", None),
            P("rows"),
            P("rows", "vocab"),
        ),
        out_specs=(P("rows", None, "vocab"), P("rows", None, "vocab")),
        check_vma=False,
    )
```

time: 583 us -> 202 us (0.35)
  waiting for transfers between devices: 363 us -> 0 us
  Pallas kernels: 0 us -> 196 us
  blocking collectives: 130 us -> 0 us
  matrix products: 39.7 us -> 0 us
  starting transfers between devices: 15 us -> 0 us
  between operations: 14.6 us -> 0.65 us
  other arithmetic: 12.8 us -> 0 us
    all_gather x2 -> x0, waiting for transfers between devices: 220 us -> none  [the longest x1 113 us: shards(): whole_head = lax.all_gather(head_weight, 'rows', axis=0, tiled=True)]
    pallas_call x0 -> x1, Pallas kernels: none -> 196 us  [shards(): pl.pallas_call(kernel, out_shape=(jax.ShapeDtypeStruct((PR, F), BF), jax....]
    reduce_scatter x1 -> x0, waiting for transfers between devices: 142 us -> none  [shards(): lax.psum_scatter(partial_terms.astype(jnp.bfloat16), 'vocab', scatter_dim...]
    all_gather x2 -> x0, blocking collectives: 58 us -> none  [the longest x1 35.3 us: shards(): lax.all_gather(hidden_query, 'vocab', axis=2, tiled=True)]
    unnamed x1 -> x0, blocking collectives: 45 us -> none
    dot_general x5 -> x0, matrix products: 39.7 us -> none  [the longest x1 20.2 us: shards(): lax.dot_general(slopes, whole_head, (((1,), (1,)), ((), ())), preferred_e...]
    psum x1 -> x0, blocking collectives: 27.5 us -> none  [shards(): scores = lax.psum(partial_scores, 'vocab') * scaling]
    unnamed x4 -> x0, starting transfers between devices: 14.9 us -> none
  transfers between devices with their start and end apart: 7 -> 0, of which waited for: 3 -> 0; matrix products, arithmetic and copies ran while one was open for 1% -> 0% of each run, Pallas kernels for 0% -> 0%
where the time goes in v1:
time: 202 us; the launch traced here: 201 us
  Pallas kernels  196 us (97%)
  local copies, waits for them, and re-layouts  4.1 us (2%)
    pallas_call x1, Pallas kernels, shards(): pl.pallas_call(kernel, out_shape=(jax.ShapeDtypeStruct((PR, F), BF), jax....  196 us
    unnamed x5, local copies, waits for them, and re-layouts  4.1 us

profile of v1, /device:TPU:1, one launch (start us, length us, event | category | flops | bytes accessed | tf_op | source)
XLA Modules:
  0.0 200.9 jit_solution(15468963145337450215)
XLA Ops:
  0.6 1.4 copy.8.mq_ref
  2.0 196.2 %step.1 = (bf16[768,512]{1,0:T(8,128)(2,1)}, bf16[96,512]{1,0:T(8,128)(2,1)}) custom-call(bf16[768,512]{1,0:T(8,128)(2,1)} %bitcast.4, bf16[96,512]{1,0:T(8,128)(2,1)} %bitcast.6, s32[12,64]{1,0:T(8,128)} %mp_ref.1, s32[12,8]{1,0:T(8,128)} %copy.8.mq_ref, s32[12]{0:T(128)} %lab_ref.1, bf16[256,2048]{1,0:T(8,128)(2,1)} %hw_ref.1), custom_call_target="tpu_custom_call" | custom-call | tf_op jit(solution)/shard_map/step/pallas_call | solution.py:462
  198.2 0.0 copy-start
  198.2 2.1 %copy.11 = bf16[12,64,512]{2,1,0:T(8,128)(2,1)} copy(bf16[12,64,512]{2,1,0:T(8,128)(2,1)} %bitcast.5) | data formatting | bytes 1572864
  200.3 0.0 copy-done
  200.3 0.6 copy.12
Async XLA Ops:
  198.2 2.1 %copy-start = (bf16[96,512]{1,0:T(8,128)(2,1)S(1)}, bf16[96,512]{1,0:T(8,128)(2,1)}, u32[]{:S(2)}) copy-start(bf16[96,512]{1,0:T(8,128)(2,1)} %get-tuple-element.5) | copy-start | bytes 294916

commit v2 on v1

--- a/solution.py
+++ b/solution.py
@@ -18,10 +18,16 @@
 QR = G * LQ
 R = PR + QR
 RH = R // 2
+ZR = 480
+ZH = ((0, 240), (240, 240))
+YR = R - ZR
+YH = ((480, 192), (672, 192))
 F = 512
 W = 2048
 HD = 256
 HH = HD // 2
+HY = 96
+HX = HD - 2 * HY
 PAD = 16
 ROWS = 16
 VOCAB = 8
@@ -63,6 +69,7 @@
     rhalf,
     rfull,
     ybuf,
+    yb,
     lsem,
     ssem,
     rsem,
@@ -90,9 +97,9 @@
     for copy in local:
         copy.start()
 
-    peers = [device(zs[d], yls[e], yh, x, c) for d, e in RELATIVE]
-    peers += [device(z, yl, yhs[e], xs[d], c) for d, e in RELATIVE]
-    peers += [device(z, yl, yhs[e], xs[d], 1 - c) for d, e in [(0, 0)] + RELATIVE]
+    acc[...] = jnp.zeros_like(acc)
+    totals[...] = jnp.zeros_like(totals)
+    peers = [zdev[1], zdev[3], yldev, xdev[1], xdev[3], yhdev, cdev]
     barrier = pltpu.get_barrier_semaphore()
     for peer in peers:
         pl.semaphore_signal(barrier, inc=1, device_id=peer, device_id_type=MESH)
@@ -125,9 +132,12 @@
     def hid(dz, dy, h):
         return tok.at[zs[dz] * 2 + yls[dy], pl.ds(h * RH, RH)]
 
-    def hed(dx, dy, h):
-        return head.at[yhs[dy] * 4 + xs[dx], pl.ds(c * HD + h * HH, HH)]
-
+    def hed(dx, dy, lo, n):
+        return head.at[yhs[dy] * 4 + xs[dx], pl.ds(c * HD + lo, n)]
+
+    halves = ((0, HH), (HH, HH))
+    ring = ((0, HY), (HY, HY))
+    rest = (2 * HY, HX)
     a, b, s = {}, {}, {}
     tok_sent = []
 
@@ -136,117 +146,128 @@
         a[key] = copy
         tok_sent.append(copy)
 
-    def b_send(key, ref, dev):
-        b[key] = send(ref, dev)
-
-    def to_core(dx, dy, h):
-        s[(dx, dy, h)] = send(hed(dx, dy, h), cdev)
+    def b_send(key, dx, dy, part, dev):
+        b[key] = send(hed(dx, dy, *part), dev)
+
+    def to_core(dx, dy, part):
+        s.setdefault((dx, dy), []).append(send(hed(dx, dy, *part), cdev))
+
+    def b_took(key, dx, dy, part):
+        b[key].wait_recv()
+        to_core(dx, dy, part)
 
     a_send(("y", 0), hid(0, 0, 0), yldev)
-    b_send(("y", 0), hed(0, 0, 0), yhdev)
     a_send(("+", 0), hid(0, 0, 0), zdev[1])
     a_send(("-", 1), hid(0, 0, 1), zdev[3])
-    b_send(("+", 0), hed(0, 0, 0), xdev[1])
-    b_send(("-", 1), hed(0, 0, 1), xdev[3])
+    b_send(("+", 0), 0, 0, halves[0], xdev[1])
+    b_send(("-", 1), 0, 0, halves[1], xdev[3])
     a_send(("y", 1), hid(0, 0, 1), yldev)
-    b_send(("y", 1), hed(0, 0, 1), yhdev)
+    b_send(("y", 0), 0, 0, ring[0], yhdev)
+    b_send(("y", 1), 0, 0, ring[1], yhdev)
     a_send(("+", 1), hid(0, 0, 1), zdev[1])
     a_send(("-", 0), hid(0, 0, 0), zdev[3])
-    b_send(("+", 1), hed(0, 0, 1), xdev[1])
-    b_send(("-", 0), hed(0, 0, 0), xdev[3])
-    to_core(0, 0, 0)
-    to_core(0, 0, 1)
+    b_send(("+", 1), 0, 0, halves[1], xdev[1])
+    b_send(("-", 0), 0, 0, halves[0], xdev[3])
+    b_send(("r", 0), 0, 0, rest, yhdev)
+    to_core(0, 0, halves[0])
+    to_core(0, 0, halves[1])
 
     a[("+", 0)].wait_recv()
     a_send("f+", hid(3, 0, 0), zdev[1])
     a[("-", 1)].wait_recv()
     a_send("f-", hid(1, 0, 1), zdev[3])
-    b[("+", 0)].wait_recv()
-    b_send("f+", hed(3, 0, 0), xdev[1])
-    b[("-", 1)].wait_recv()
-    b_send("f-", hed(1, 0, 1), xdev[3])
-    to_core(3, 0, 0)
-    to_core(1, 0, 1)
+    b_took(("+", 0), 3, 0, halves[0])
+    b_send("f+", 3, 0, halves[0], xdev[1])
+    b_took(("-", 1), 1, 0, halves[1])
+    b_send("f-", 1, 0, halves[1], xdev[3])
+    b_send(("r", 1), 1, 0, rest, yhdev)
 
     a[("y", 0)].wait_recv()
     a_send(("o+", 0), hid(0, 1, 0), zdev[1])
-    a_send(("o-", 0), hid(0, 1, 0), zdev[3])
-    b[("y", 0)].wait_recv()
-    b_send(("o+", 0), hed(0, 1, 0), xdev[1])
-    b_send(("o-", 0), hed(0, 1, 0), xdev[3])
+    b_took(("+", 1), 3, 0, halves[1])
+    b_send(("r", 3), 3, 0, rest, yhdev)
+    b_took(("-", 0), 1, 0, halves[0])
     a[("y", 1)].wait_recv()
     a_send(("o-", 1), hid(0, 1, 1), zdev[3])
+    a_send(("o-", 0), hid(0, 1, 0), zdev[3])
     a_send(("o+", 1), hid(0, 1, 1), zdev[1])
-    b[("y", 1)].wait_recv()
-    b_send(("o-", 1), hed(0, 1, 1), xdev[3])
-    b_send(("o+", 1), hed(0, 1, 1), xdev[1])
-    to_core(0, 1, 0)
-    to_core(0, 1, 1)
-    b[("+", 1)].wait_recv()
-    to_core(3, 0, 1)
-    b[("-", 0)].wait_recv()
-    to_core(1, 0, 0)
+    b_took(("y", 0), 0, 1, ring[0])
+    b_send(("o+", 0), 0, 1, ring[0], xdev[1])
+    b_took(("y", 1), 0, 1, ring[1])
+    b_send(("o-", 1), 0, 1, ring[1], xdev[3])
+    b_send(("o-", 0), 0, 1, ring[0], xdev[3])
+    b_send(("o+", 1), 0, 1, ring[1], xdev[1])
+    b_took("f+", 2, 0, halves[0])
+    b_took("f-", 2, 0, halves[1])
+    b_send(("r", 2), 2, 0, rest, yhdev)
+
+    def core_took(dx, dy):
+        for copy in s[(dx, dy)]:
+            copy.wait_recv()
+
+    def mm1(ready):
+        @pl.loop(0, VOCAB)
+        def _(slot):
+            @pl.when(ready(slot))
+            def _():
+                @pl.loop(0, 2)
+                def _(n):
+                    cols = pl.ds(pl.multiple_of(n * (W // 2), W // 2), W // 2)
+                    acc[:, cols] += jnp.dot(
+                        tok[slot], head[slot, :, cols], preferred_element_type=F32
+                    )
+
+    def near_head(slot):
+        return slot // 4 == yh
+
+    def near_hidden(slot):
+        return slot % 2 == yl
+
+    def far(slot):
+        return (jnp.logical_not(near_head(slot)) & (slot % 4 == xs[2])) | (
+            jnp.logical_not(near_hidden(slot)) & (slot // 2 == zs[2])
+        )
+
+    for key in [("+", 1), ("-", 0), "f+", "f-"]:
+        a[key].wait_recv()
+    for dx in range(4):
+        core_took(dx, 0)
+    mm1(lambda slot: near_head(slot) & near_hidden(slot))
     a[("o+", 0)].wait_recv()
     a_send("g+", hid(3, 1, 0), zdev[1])
-    b[("o+", 0)].wait_recv()
-    b_send("g+", hed(3, 1, 0), xdev[1])
-    to_core(3, 1, 0)
     a[("o-", 1)].wait_recv()
     a_send("g-", hid(1, 1, 1), zdev[3])
-    b[("o-", 1)].wait_recv()
-    b_send("g-", hed(1, 1, 1), xdev[3])
-    to_core(1, 1, 1)
-    b["f+"].wait_recv()
-    to_core(2, 0, 0)
-    b["f-"].wait_recv()
-    to_core(2, 0, 1)
-    for key in [("+", 1), ("-", 0), "f+", "f-", ("o-", 0), ("o+", 1), "g+", "g-"]:
-        a[key].wait_recv()
-
-    def mm1(dx, dy, first):
-        slot = yhs[dy] * 4 + xs[dx]
-        for h in (0, 1):
-            s[(dx, dy, h)].wait_recv()
-
-        @pl.loop(0, W // 256)
-        def _(n):
-            cols = pl.ds(pl.multiple_of(n * 256, 256), 256)
-            product = jnp.dot(tok[slot], head[slot, :, cols], preferred_element_type=F32)
-            if first:
-                acc[:, cols] = product
-            else:
-                acc[:, cols] += product
-
-    mm1(0, 0, True)
-    mm1(1, 0, False)
-    mm1(3, 0, False)
-    b[("o+", 1)].wait_recv()
-    to_core(3, 1, 1)
-    b[("o-", 0)].wait_recv()
-    to_core(1, 1, 0)
-    mm1(0, 1, False)
-    mm1(2, 0, False)
-    mm1(1, 1, False)
-    mm1(3, 1, False)
-    b["g+"].wait_recv()
-    to_core(2, 1, 0)
-    b["g-"].wait_recv()
-    to_core(2, 1, 1)
-    mm1(2, 1, False)
-
-    totals[...] = jnp.zeros_like(totals)
-
-    def pool(base, length, mask_ref, k, side):
+    b_took(("o+", 0), 3, 1, ring[0])
+    b_send("g+", 3, 1, ring[0], xdev[1])
+    b_took(("o-", 1), 1, 1, ring[1])
+    b_send("g-", 1, 1, ring[1], xdev[3])
+    a[("o+", 1)].wait_recv()
+    a[("o-", 0)].wait_recv()
+    b_took(("r", 0), 0, 1, rest)
+    mm1(
+        lambda slot: near_head(slot)
+        & jnp.logical_not(near_hidden(slot))
+        & jnp.logical_not(far(slot))
+    )
+    b_took(("o+", 1), 3, 1, ring[1])
+    b_took(("o-", 0), 1, 1, ring[0])
+    b_took(("r", 1), 1, 1, rest)
+    b_took(("r", 3), 3, 1, rest)
+    for dx in (0, 1, 3):
+        core_took(dx, 1)
+    mm1(lambda slot: jnp.logical_not(near_head(slot)) & jnp.logical_not(far(slot)))
+    b_took(("r", 2), 2, 1, rest)
+    b_took("g+", 2, 1, ring[0])
+    b_took("g-", 2, 1, ring[1])
+    a["g+"].wait_recv()
+    a["g-"].wait_recv()
+    core_took(2, 1)
+    mm1(far)
+
+    def pool(base, length, weight, k, side, first):
         rows = pl.ds(pl.multiple_of(base + k * length, 8), length)
-        line = mask_ref[pl.ds(k, 1), :].astype(F32)
-        eye = lax.broadcasted_iota(jnp.int32, (length, length), 0) == lax.broadcasted_iota(
-            jnp.int32, (length, length), 1
-        )
-        weight = jnp.sum(
-            jnp.where(eye, jnp.broadcast_to(line, (length, length)), 0.0), axis=1, keepdims=True
-        )
-        for n in range(W // 256):
-            cols = pl.ds(n * 256, 256)
+        for n in range(first, first + W // 2, 256):
+            cols = pl.ds(n, 256)
             high = jnp.maximum(acc[rows, cols], 0.0)
             act = jnp.log1p(high)
             square = act * act
@@ -255,34 +276,57 @@
             )
             acc[rows, cols] = weight * (square * act) / (1.0 + high)
 
-    @pl.loop(0, G)
-    def _(k):
-        pool(0, LP, mp_ref, k, 0)
-        pool(PR, LQ, mq_ref, k, 1)
+    def line_weight(k):
+        line = mp_ref[pl.ds(k, 1), :].astype(F32)
+        shape = (LP, LP)
+        eye = lax.broadcasted_iota(jnp.int32, shape, 0) == lax.broadcasted_iota(jnp.int32, shape, 1)
+        return jnp.sum(jnp.where(eye, jnp.broadcast_to(line, shape), 0.0), axis=1, keepdims=True)
+
+    def query_weight(k):
+        shape = (LQ, G)
+        here = lax.broadcasted_iota(jnp.int32, shape, 1) == k
+        return jnp.sum(jnp.where(here, mq_ref[...].astype(F32), 0.0), axis=1, keepdims=True)
 
     def fourth_root(t):
         return jnp.sqrt(jnp.sqrt(t))
 
-    allp[r] = (fourth_root(totals[0] + 1.0) - 1.0).astype(BF)
-    allq[r] = (fourth_root(totals[1] + 1.0) - 1.0).astype(BF)
-
-    def spread(ref):
-        copies = [send(ref.at[r], device(z, yl, yhs[e], xs[d], c)) for d, e in RELATIVE]
-        copies.append(send(ref.at[r], cdev))
+    def spread(ref, cols):
+        mine = ref.at[r, :, cols]
+        copies = [send(mine, device(z, yl, yhs[e], xs[d], c)) for d, e in RELATIVE]
+        copies.append(send(mine, cdev))
         return copies
 
-    def hand_on(ref, copies):
+    def hand_on(ref, cols, copies):
         handed = []
         for (d, e), copy in zip(RELATIVE, copies):
             copy.wait_recv()
             came = (yhs[e] * 4 + xs[(4 - d) % 4]) * 2 + c
-            handed.append(send(ref.at[came], cdev))
+            handed.append(send(ref.at[came, :, cols], cdev))
         return handed
 
-    spread_p = spread(allp)
-    spread_q = spread(allq)
-    handed_p = hand_on(allp, spread_p)
-    spread_p[7].wait_recv()
+    spread_p = []
+    for first in (0, W // 2):
+        cols = pl.ds(first, W // 2)
+
+        @pl.loop(0, G)
+        def _(k):
+            pool(0, LP, line_weight(k), k, 0, first)
+
+        allp[r, :, cols] = (fourth_root(totals[0, :, cols] + 1.0) - 1.0).astype(BF)
+        spread_p.append((cols, spread(allp, cols)))
+
+    @pl.loop(0, G)
+    def _(k):
+        pool(PR, LQ, query_weight(k), k, 1, 0)
+        pool(PR, LQ, query_weight(k), k, 1, W // 2)
+
+    whole = pl.ds(0, W)
+    allq[r] = (fourth_root(totals[1] + 1.0) - 1.0).astype(BF)
+    handed_p = []
+    for cols, copies in spread_p:
+        handed_p += hand_on(allp, cols, copies)
+        handed_p.append(copies[7])
+    spread_q = spread(allq, whole)
     for copy in handed_p:
         copy.wait_recv()
 
@@ -291,7 +335,6 @@
         allq[r], every_pass, (((1,), (1,)), ((), ())), preferred_element_type=F32
     )
     shared = [send(sbuf.at[v], device(zs[d], yls[e], yh, x, c)) for d, e in RELATIVE]
-    handed_q = hand_on(allq, spread_q)
     row_at = lax.broadcasted_iota(jnp.int32, (PAD, ROWS * PAD), 0)
     col_at = lax.broadcasted_iota(jnp.int32, (PAD, ROWS * PAD), 1)
     passage = (col_at // PAD) * G + col_at % PAD
@@ -336,6 +379,7 @@
         )
         slopes[rows, :] = (acc[rows, :] * gain).astype(BF)
 
+    handed_q = hand_on(allq, whole, spread_q)
     spread_q[7].wait_recv()
     for copy in handed_q:
         copy.wait_recv()
@@ -366,6 +410,9 @@
     for copy in tok_sent:
         copy.wait_send()
 
+    def part(dz, dy, lo, n):
+        return tok.at[zs[dz] * 2 + yls[dy], pl.ds(lo, n)]
+
     def mm2(dz, dy):
         slot = zs[dz] * 2 + yls[dy]
 
@@ -379,58 +426,97 @@
                 preferred_element_type=F32,
             ).astype(BF)
 
-    def add_into(slot, h, other):
-        @pl.loop(0, RH // 48)
+    def add_into(dz, dy, lo, size, *others):
+        slot = zs[dz] * 2 + yls[dy]
+
+        @pl.loop(0, size // 48)
         def _(k):
-            rows = pl.ds(pl.multiple_of(h * RH + k * 48, 16), 48)
-            some = pl.ds(pl.multiple_of(k * 48, 16), 48)
-            tok[slot, rows, :] = (
-                tok[slot, rows, :].astype(F32) + other[some, :].astype(F32)
-            ).astype(BF)
+            rows = pl.ds(pl.multiple_of(lo + k * 48, 16), 48)
+            total = tok[slot, rows, :].astype(F32)
+            for other in others:
+                total = total + other[rows, :].astype(F32)
+            tok[slot, rows, :] = total.astype(BF)
 
     def out(src, dst, dev):
         copy = remote(src, dst, dev)
         sent.append(copy)
         return copy
 
-    arrivals = {}
-    for dy in (1, 0):
-        mm2(2, dy)
-        up = out(hid(2, dy, 0), rhalf.at[dy, 0], zdev[1])
-        down = out(hid(2, dy, 1), rhalf.at[dy, 1], zdev[3])
-        mm2(1, dy)
-        arrivals[(dy, 0, 1)] = out(hid(1, dy, 1), rfull.at[dy, 0, pl.ds(RH, RH)], zdev[1])
-        mm2(3, dy)
-        arrivals[(dy, 1, 0)] = out(hid(3, dy, 0), rfull.at[dy, 1, pl.ds(0, RH)], zdev[3])
-        up.wait_recv()
-        add_into(zs[1] * 2 + yls[dy], 0, rhalf.at[dy, 0])
-        arrivals[(dy, 0, 0)] = out(hid(1, dy, 0), rfull.at[dy, 0, pl.ds(0, RH)], zdev[1])
-        down.wait_recv()
-        add_into(zs[3] * 2 + yls[dy], 1, rhalf.at[dy, 1])
-        arrivals[(dy, 1, 1)] = out(hid(3, dy, 1), rfull.at[dy, 1, pl.ds(RH, RH)], zdev[3])
+    def to_ring(dz, dy, lo, n, ref):
+        dev = zdev[1] if ref == 0 else zdev[3]
+        return out(part(dz, dy, lo, n), rfull.at[dy, ref, pl.ds(lo, n)], dev)
+
+    def to_half(dy, lo, n, ref):
+        dev = zdev[1] if ref == 0 else zdev[3]
+        return out(part(2, dy, lo, n), rhalf.at[dy, ref, pl.ds(lo, n)], dev)
+
+    def to_pair(dz):
+        return out(part(dz, 1, ZR, YR), yb.at[dz], yldev)
+
+    mm2(2, 1)
+    up = to_half(1, *ZH[0], 0)
+    down = to_half(1, *ZH[1], 1)
+    pair = {2: to_pair(2)}
+    mm2(1, 1)
+    other_plane = [to_ring(1, 1, *ZH[1], 0)]
+    pair[1] = to_pair(1)
+    mm2(3, 1)
+    other_plane.append(to_ring(3, 1, *ZH[0], 1))
+    pair[3] = to_pair(3)
+    up.wait_recv()
+    add_into(1, 1, *ZH[0], rhalf.at[1, 0])
+    other_plane.append(to_ring(1, 1, *ZH[0], 0))
+    down.wait_recv()
+    add_into(3, 1, *ZH[1], rhalf.at[1, 1])
+    other_plane.append(to_ring(3, 1, *ZH[1], 1))
     mm2(0, 1)
+    last = [out(part(0, 1, ZR, YR), ybuf.at[pl.ds(ZR, YR)], yldev)]
+
+    def add_pair(dz):
+        slot = zs[dz] * 2 + yl
+        pair[dz].wait_recv()
+
+        @pl.loop(0, YR // 48)
+        def _(k):
+            rows = pl.ds(pl.multiple_of(ZR + k * 48, 16), 48)
+            some = pl.ds(pl.multiple_of(k * 48, 16), 48)
+            tok[slot, rows, :] = (
+                tok[slot, rows, :].astype(F32) + yb[dz, some, :].astype(F32)
+            ).astype(BF)
+
+    mm2(2, 0)
+    up = to_half(0, *ZH[0], 0)
+    down = to_half(0, *ZH[1], 1)
+    add_pair(2)
+    up_y = to_half(0, *YH[0], 0)
+    down_y = to_half(0, *YH[1], 1)
+    mm2(1, 0)
+    last.append(to_ring(1, 0, *ZH[1], 0))
+    mm2(3, 0)
+    last.append(to_ring(3, 0, *ZH[0], 1))
+    for copy in other_plane:
+        copy.wait_recv()
+    add_into(0, 1, 0, ZR, rfull.at[1, 0], rfull.at[1, 1])
+    last.append(out(part(0, 1, 0, ZR), ybuf.at[pl.ds(0, ZR)], yldev))
+    up.wait_recv()
+    add_into(1, 0, *ZH[0], rhalf.at[0, 0])
+    last.append(to_ring(1, 0, *ZH[0], 0))
+    down.wait_recv()
+    add_into(3, 0, *ZH[1], rhalf.at[0, 1])
+    last.append(to_ring(3, 0, *ZH[1], 1))
+    add_pair(1)
+    last.append(to_ring(1, 0, *YH[1], 0))
+    add_pair(3)
+    last.append(to_ring(3, 0, *YH[0], 1))
     mm2(0, 0)
-
-    slot = z * 2 + (1 - yl)
-    across = []
-    for h in (0, 1):
-        arrivals[(1, 0, h)].wait_recv()
-        arrivals[(1, 1, h)].wait_recv()
-
-        @pl.loop(0, RH // 48)
-        def _(k):
-            rows = pl.ds(pl.multiple_of(h * RH + k * 48, 16), 48)
-            tok[slot, rows, :] = (
-                tok[slot, rows, :].astype(F32)
-                + rfull[1, 0, rows, :].astype(F32)
-                + rfull[1, 1, rows, :].astype(F32)
-            ).astype(BF)
-
-        across.append(out(hid(0, 1, h), ybuf.at[pl.ds(h * RH, RH)], yldev))
-    for copy in across:
+    up_y.wait_recv()
+    add_into(1, 0, *YH[0], rhalf.at[0, 0])
+    last.append(to_ring(1, 0, *YH[0], 0))
+    down_y.wait_recv()
+    add_into(3, 0, *YH[1], rhalf.at[0, 1])
+    last.append(to_ring(3, 0, *YH[1], 1))
+    for copy in last:
         copy.wait_recv()
-    for key in [(0, 0, 0), (0, 0, 1), (0, 1, 0), (0, 1, 1)]:
-        arrivals[key].wait_recv()
 
     def total(rows):
         return (
@@ -452,7 +538,7 @@
         copy.wait_send()
 
 
-COPIES = 150
+COPIES = 192
 
 
 def shards(hidden_pass, hidden_query, mask_pass, mask_query, labels, head_weight):
@@ -478,9 +564,10 @@
             pltpu.VMEM((ROWS, PAD, W), BF),
             pltpu.VMEM((VOCAB, PAD, ROWS * PAD), F32),
             pltpu.VMEM((ROWS, PAD, ROWS * PAD), BF),
-            pltpu.VMEM((2, 2, RH, F), BF),
+            pltpu.VMEM((2, 2, R, F), BF),
             pltpu.VMEM((2, 2, R, F), BF),
             pltpu.VMEM((R, F), BF),
+            pltpu.VMEM((4, YR, F), BF),
             pltpu.SemaphoreType.DMA((3,)),
             pltpu.SemaphoreType.DMA((COPIES,)),
             pltpu.SemaphoreType.DMA((COPIES,)),
@@ -493,7 +580,7 @@
         hidden_pass.reshape(PR, F),
         hidden_query.reshape(QR, F),
         mask_pass,
-        mask_query,
+        mask_query.T,
         labels,
         head_weight,
     )

time: 202 us -> 166 us (0.82)
  Pallas kernels: 196 us -> 163 us
    pallas_call x1, Pallas kernels: 196 us -> 163 us  [shards(): pl.pallas_call(kernel, out_shape=(jax.ShapeDtypeStruct((PR, F), BF), jax....]
    unnamed x5 -> x4, local copies, waits for them, and re-layouts: 4.1 us -> 2.74 us
where the time goes in v2:
time: 166 us
  Pallas kernels  163 us (98%)
  local copies, waits for them, and re-layouts  2.74 us (2%)
    pallas_call x1, Pallas kernels, shards(): pl.pallas_call(kernel, out_shape=(jax.ShapeDtypeStruct((PR, F), BF), jax....  163 us

profile of v2, /device:TPU:1, one launch (start us, length us, event | category | flops | bytes accessed | tf_op | source)
XLA Modules:
  0.0 166.3 jit_solution(2342507065653994609)
XLA Ops:
  0.6 162.9 %step.1 = (bf16[768,512]{1,0:T(8,128)(2,1)}, bf16[96,512]{1,0:T(8,128)(2,1)}) custom-call(bf16[768,512]{1,0:T(8,128)(2,1)} %bitcast.5, bf16[96,512]{1,0:T(8,128)(2,1)} %bitcast.7, s32[12,64]{1,0:T(8,128)} %mp_ref.1, s32[8,12]{1,0:T(8,128)} %bitcast.9, s32[12]{0:T(128)} %lab_ref.1, bf16[256,2048]{1,0:T(8,128)(2,1)} %hw_ref.1), custom_call_target="tpu_custom_call" | custom-call | tf_op jit(solution)/shard_map/step/pallas_call | solution.py:548
  163.6 0.0 copy-start
  163.6 2.1 %copy.10 = bf16[12,64,512]{2,1,0:T(8,128)(2,1)} copy(bf16[12,64,512]{2,1,0:T(8,128)(2,1)} %bitcast.6) | data formatting | bytes 1572864
  165.7 0.0 copy-done
  165.7 0.6 copy.11
Async XLA Ops:
  163.6 2.1 %copy-start = (bf16[96,512]{1,0:T(8,128)(2,1)S(1)}, bf16[96,512]{1,0:T(8,128)(2,1)}, u32[]{:S(2)}) copy-start(bf16[96,512]{1,0:T(8,128)(2,1)} %get-tuple-element.5) | copy-start | bytes 294916

commit v3 on v2

--- a/solution.py
+++ b/solution.py
@@ -176,11 +176,13 @@
     a_send("f+", hid(3, 0, 0), zdev[1])
     a[("-", 1)].wait_recv()
     a_send("f-", hid(1, 0, 1), zdev[3])
-    b_took(("+", 0), 3, 0, halves[0])
+    b[("+", 0)].wait_recv()
     b_send("f+", 3, 0, halves[0], xdev[1])
-    b_took(("-", 1), 1, 0, halves[1])
+    b[("-", 1)].wait_recv()
     b_send("f-", 1, 0, halves[1], xdev[3])
     b_send(("r", 1), 1, 0, rest, yhdev)
+    to_core(3, 0, halves[0])
+    to_core(1, 0, halves[1])
 
     a[("y", 0)].wait_recv()
     a_send(("o+", 0), hid(0, 1, 0), zdev[1])
@@ -191,12 +193,14 @@
     a_send(("o-", 1), hid(0, 1, 1), zdev[3])
     a_send(("o-", 0), hid(0, 1, 0), zdev[3])
     a_send(("o+", 1), hid(0, 1, 1), zdev[1])
-    b_took(("y", 0), 0, 1, ring[0])
+    b[("y", 0)].wait_recv()
     b_send(("o+", 0), 0, 1, ring[0], xdev[1])
-    b_took(("y", 1), 0, 1, ring[1])
+    b[("y", 1)].wait_recv()
     b_send(("o-", 1), 0, 1, ring[1], xdev[3])
     b_send(("o-", 0), 0, 1, ring[0], xdev[3])
     b_send(("o+", 1), 0, 1, ring[1], xdev[1])
+    to_core(0, 1, ring[0])
+    to_core(0, 1, ring[1])
     b_took("f+", 2, 0, halves[0])
     b_took("f-", 2, 0, halves[1])
     b_send(("r", 2), 2, 0, rest, yhdev)
@@ -223,10 +227,14 @@
     def near_hidden(slot):
         return slot % 2 == yl
 
+    def far_head(slot):
+        return jnp.logical_not(near_head(slot)) & (slot % 4 == xs[2])
+
+    def far_hidden(slot):
+        return jnp.logical_not(near_hidden(slot)) & (slot // 2 == zs[2])
+
     def far(slot):
-        return (jnp.logical_not(near_head(slot)) & (slot % 4 == xs[2])) | (
-            jnp.logical_not(near_hidden(slot)) & (slot // 2 == zs[2])
-        )
+        return far_head(slot) | far_hidden(slot)
 
     for key in [("+", 1), ("-", 0), "f+", "f-"]:
         a[key].wait_recv()
@@ -237,10 +245,12 @@
     a_send("g+", hid(3, 1, 0), zdev[1])
     a[("o-", 1)].wait_recv()
     a_send("g-", hid(1, 1, 1), zdev[3])
-    b_took(("o+", 0), 3, 1, ring[0])
+    b[("o+", 0)].wait_recv()
     b_send("g+", 3, 1, ring[0], xdev[1])
-    b_took(("o-", 1), 1, 1, ring[1])
+    b[("o-", 1)].wait_recv()
     b_send("g-", 1, 1, ring[1], xdev[3])
+    to_core(3, 1, ring[0])
+    to_core(1, 1, ring[1])
     a[("o+", 1)].wait_recv()
     a[("o-", 0)].wait_recv()
     b_took(("r", 0), 0, 1, rest)
@@ -256,13 +266,14 @@
     for dx in (0, 1, 3):
         core_took(dx, 1)
     mm1(lambda slot: jnp.logical_not(near_head(slot)) & jnp.logical_not(far(slot)))
+    a["g+"].wait_recv()
+    a["g-"].wait_recv()
     b_took(("r", 2), 2, 1, rest)
+    mm1(lambda slot: far_hidden(slot) & jnp.logical_not(far_head(slot)))
     b_took("g+", 2, 1, ring[0])
     b_took("g-", 2, 1, ring[1])
-    a["g+"].wait_recv()
-    a["g-"].wait_recv()
     core_took(2, 1)
-    mm1(far)
+    mm1(far_head)
 
     def pool(base, length, weight, k, side, first):
         rows = pl.ds(pl.multiple_of(base + k * length, 8), length)
@@ -274,7 +285,14 @@
             totals[side, pl.ds(k, 1), cols] = jnp.sum(
                 square * square * weight, axis=0, keepdims=True
             )
-            acc[rows, cols] = weight * (square * act) / (1.0 + high)
+
+    def slope(base, length, weight, k):
+        rows = pl.ds(pl.multiple_of(base + k * length, 8), length)
+        for n in range(0, W, 256):
+            cols = pl.ds(n, 256)
+            high = jnp.maximum(acc[rows, cols], 0.0)
+            act = jnp.log1p(high)
+            acc[rows, cols] = weight * (act * act * act) / (1.0 + high)
 
     def line_weight(k):
         line = mp_ref[pl.ds(k, 1), :].astype(F32)
@@ -322,6 +340,11 @@
 
     whole = pl.ds(0, W)
     allq[r] = (fourth_root(totals[1] + 1.0) - 1.0).astype(BF)
+
+    @pl.loop(0, G)
+    def _(k):
+        slope(0, LP, line_weight(k), k)
+
     handed_p = []
     for cols, copies in spread_p:
         handed_p += hand_on(allp, cols, copies)
@@ -335,6 +358,11 @@
         allq[r], every_pass, (((1,), (1,)), ((), ())), preferred_element_type=F32
     )
     shared = [send(sbuf.at[v], device(zs[d], yls[e], yh, x, c)) for d, e in RELATIVE]
+
+    @pl.loop(0, G)
+    def _(k):
+        slope(PR, LQ, query_weight(k), k)
+
     row_at = lax.broadcasted_iota(jnp.int32, (PAD, ROWS * PAD), 0)
     col_at = lax.broadcasted_iota(jnp.int32, (PAD, ROWS * PAD), 1)
     passage = (col_at // PAD) * G + col_at % PAD
@@ -402,10 +430,11 @@
     )
     factor[0] = pass_grad * tail(totals[0] + 1.0)
 
-    @pl.loop(0, G)
-    def _(k):
-        rows = pl.ds(pl.multiple_of(k * LP, LP), LP)
-        slopes[rows, :] = (acc[rows, :] * factor[0, pl.ds(k, 1), :]).astype(BF)
+    def pass_slopes(lo, n):
+        @pl.loop(lo // 16, (lo + n) // 16)
+        def _(k):
+            rows = pl.ds(pl.multiple_of(k * 16, 16), 16)
+            slopes[rows, :] = (acc[rows, :] * factor[0, pl.ds(k // (LP // 16), 1), :]).astype(BF)
 
     for copy in tok_sent:
         copy.wait_send()
@@ -426,6 +455,16 @@
                 preferred_element_type=F32,
             ).astype(BF)
 
+    def mm2_rows(dz, dy, lo, n):
+        slot = zs[dz] * 2 + yls[dy]
+        rows = pl.ds(lo, n)
+        tok[slot, rows, :] = lax.dot_general(
+            slopes[rows, :],
+            head[slot],
+            (((1,), (1,)), ((), ())),
+            preferred_element_type=F32,
+        ).astype(BF)
+
     def add_into(dz, dy, lo, size, *others):
         slot = zs[dz] * 2 + yls[dy]
 
@@ -453,9 +492,14 @@
     def to_pair(dz):
         return out(part(dz, 1, ZR, YR), yb.at[dz], yldev)
 
-    mm2(2, 1)
+    pass_slopes(*ZH[0])
+    mm2_rows(2, 1, *ZH[0])
     up = to_half(1, *ZH[0], 0)
+    pass_slopes(*ZH[1])
+    mm2_rows(2, 1, *ZH[1])
     down = to_half(1, *ZH[1], 1)
+    pass_slopes(ZR, PR - ZR)
+    mm2_rows(2, 1, ZR, YR)
     pair = {2: to_pair(2)}
     mm2(1, 1)
     other_plane = [to_ring(1, 1, *ZH[1], 0)]
@@ -573,7 +617,7 @@
             pltpu.SemaphoreType.DMA((COPIES,)),
         ],
         compiler_params=pltpu.CompilerParams(
-            collective_id=0, has_side_effects=True, vmem_limit_bytes=60 * 1024 * 1024
+            collective_id=0, has_side_effects=True, vmem_limit_bytes=52 * 1024 * 1024
         ),
         name="step",
     )(

time: 166 us -> 167 us (level)
  local copies, waits for them, and re-layouts: 2.74 us -> 4.92 us
  Pallas kernels: 163 us -> 161 us
    unnamed x4 -> x12, local copies, waits for them, and re-layouts: 2.74 us -> 4.92 us
    pallas_call x1, Pallas kernels: 163 us -> 161 us  [shards(): pl.pallas_call(kernel, out_shape=(jax.ShapeDtypeStruct((PR, F), BF), jax....]
where the time goes in v3:
time: 167 us; the launch traced here: 166 us
  Pallas kernels  161 us (96%)
  local copies, waits for them, and re-layouts  4.92 us (3%)
    pallas_call x1, Pallas kernels, shards(): pl.pallas_call(kernel, out_shape=(jax.ShapeDtypeStruct((PR, F), BF), jax....  161 us
    unnamed x12, local copies, waits for them, and re-layouts  4.92 us

profile of v3, /device:TPU:1, one launch (start us, length us, event | category | flops | bytes accessed | tf_op | source)
XLA Modules:
  0.0 166.3 jit_solution(18167391874190476219)
XLA Ops:
  0.6 0.0 copy-start.3
  0.6 0.0 copy-start.4
  0.7 0.7 copy-done.3
  1.3 0.0 copy-done.4
  1.3 0.0 copy-start
  1.3 1.1 copy-done
  2.5 0.0 copy-start.1
  2.5 0.9 copy-done.1
  3.3 0.0 copy-start.2
  3.4 0.7 copy-done.2
  4.0 160.8 %step.1 = (bf16[768,512]{1,0:T(8,128)(2,1)S(1)}, bf16[96,512]{1,0:T(8,128)(2,1)S(1)}) custom-call(bf16[768,512]{1,0:T(8,128)(2,1)S(1)} %bitcast.5, bf16[96,512]{1,0:T(8,128)(2,1)S(1)} %bitcast.7, s32[12,64]{1,0:T(8,128)S(1)} %copy-done.2, s32[8,12]{1,0:T(8,128)S(1)} %bitcast.9, s32[12]{0:T(128)S(1)} %copy-done.4, bf16[256,2048]{1,0:T(8,128)(2,1)} %hw_ref.1), custom_call_target="tpu_custom_call" | custom-call | tf_op jit(solution)/shard_map/step/pallas_call | solution.py:592
  164.8 0.9 copy.10
  165.7 0.6 copy.11
Async XLA Ops:
  0.6 0.7 copy-start.3
  0.6 0.7 copy-start.4
  1.3 1.1 copy-start
  2.5 0.9 copy-start.1
  3.3 0.7 copy-start.2

commit v4 on v3

--- a/solution.py
+++ b/solution.py
@@ -18,10 +18,10 @@
 QR = G * LQ
 R = PR + QR
 RH = R // 2
-ZR = 480
-ZH = ((0, 240), (240, 240))
+ZR = 512
+ZH = ((0, 256), (256, 256))
 YR = R - ZR
-YH = ((480, 192), (672, 192))
+YH = ((512, 176), (688, 176))
 F = 512
 W = 2048
 HD = 256
@@ -97,15 +97,13 @@
     for copy in local:
         copy.start()
 
-    acc[...] = jnp.zeros_like(acc)
-    totals[...] = jnp.zeros_like(totals)
     peers = [zdev[1], zdev[3], yldev, xdev[1], xdev[3], yhdev, cdev]
     barrier = pltpu.get_barrier_semaphore()
     for peer in peers:
         pl.semaphore_signal(barrier, inc=1, device_id=peer, device_id_type=MESH)
-    pl.semaphore_wait(barrier, len(peers))
     for copy in local:
         copy.wait()
+    pl.semaphore_wait(barrier, len(peers))
 
     counter = [0]
     sent = []
@@ -172,6 +170,9 @@
     to_core(0, 0, halves[0])
     to_core(0, 0, halves[1])
 
+    acc[...] = jnp.zeros_like(acc)
+    totals[...] = jnp.zeros_like(totals)
+
     a[("+", 0)].wait_recv()
     a_send("f+", hid(3, 0, 0), zdev[1])
     a[("-", 1)].wait_recv()
@@ -195,9 +196,10 @@
     a_send(("o+", 1), hid(0, 1, 1), zdev[1])
     b[("y", 0)].wait_recv()
     b_send(("o+", 0), 0, 1, ring[0], xdev[1])
+    b_send(("o-", 0), 0, 1, (0, HY // 2), xdev[3])
     b[("y", 1)].wait_recv()
     b_send(("o-", 1), 0, 1, ring[1], xdev[3])
-    b_send(("o-", 0), 0, 1, ring[0], xdev[3])
+    b_send(("o-", 2), 0, 1, (HY // 2, HY // 2), xdev[3])
     b_send(("o+", 1), 0, 1, ring[1], xdev[1])
     to_core(0, 1, ring[0])
     to_core(0, 1, ring[1])
@@ -254,24 +256,32 @@
     a[("o+", 1)].wait_recv()
     a[("o-", 0)].wait_recv()
     b_took(("r", 0), 0, 1, rest)
+    core_took(0, 1)
     mm1(
-        lambda slot: near_head(slot)
-        & jnp.logical_not(near_hidden(slot))
-        & jnp.logical_not(far(slot))
+        lambda slot: (
+            (near_head(slot) & jnp.logical_not(near_hidden(slot)))
+            | (slot == (1 - yh) * 4 + x)
+        )
+        & jnp.logical_not(far_hidden(slot))
     )
     b_took(("o+", 1), 3, 1, ring[1])
-    b_took(("o-", 0), 1, 1, ring[0])
+    b_took(("o-", 0), 1, 1, (0, HY // 2))
+    b_took(("o-", 2), 1, 1, (HY // 2, HY // 2))
     b_took(("r", 1), 1, 1, rest)
     b_took(("r", 3), 3, 1, rest)
-    for dx in (0, 1, 3):
+    for dx in (1, 3):
         core_took(dx, 1)
-    mm1(lambda slot: jnp.logical_not(near_head(slot)) & jnp.logical_not(far(slot)))
+    mm1(
+        lambda slot: jnp.logical_not(near_head(slot))
+        & (slot % 4 != x)
+        & jnp.logical_not(far(slot))
+    )
+    b_took(("r", 2), 2, 1, rest)
+    b_took("g+", 2, 1, ring[0])
+    b_took("g-", 2, 1, ring[1])
     a["g+"].wait_recv()
     a["g-"].wait_recv()
-    b_took(("r", 2), 2, 1, rest)
     mm1(lambda slot: far_hidden(slot) & jnp.logical_not(far_head(slot)))
-    b_took("g+", 2, 1, ring[0])
-    b_took("g-", 2, 1, ring[1])
     core_took(2, 1)
     mm1(far_head)
 
@@ -345,11 +355,11 @@
     def _(k):
         slope(0, LP, line_weight(k), k)
 
+    spread_q = spread(allq, whole)
     handed_p = []
     for cols, copies in spread_p:
         handed_p += hand_on(allp, cols, copies)
         handed_p.append(copies[7])
-    spread_q = spread(allq, whole)
     for copy in handed_p:
         copy.wait_recv()
 
@@ -388,6 +398,7 @@
     gbuf[r] = score_grad
     group = [send(gbuf.at[r], device(z, yl, yhs[e], xs[d], cs[f])) for d, e in RELATIVE for f in (0, 1)]
     group.append(send(gbuf.at[r], cdev))
+    handed_q = hand_on(allq, whole, spread_q)
 
     def tail(t):
         root = jnp.sqrt(t)
@@ -407,7 +418,6 @@
         )
         slopes[rows, :] = (acc[rows, :] * gain).astype(BF)
 
-    handed_q = hand_on(allq, whole, spread_q)
     spread_q[7].wait_recv()
     for copy in handed_q:
         copy.wait_recv()
@@ -468,9 +478,9 @@
     def add_into(dz, dy, lo, size, *others):
         slot = zs[dz] * 2 + yls[dy]
 
-        @pl.loop(0, size // 48)
+        @pl.loop(0, size // 16)
         def _(k):
-            rows = pl.ds(pl.multiple_of(lo + k * 48, 16), 48)
+            rows = pl.ds(pl.multiple_of(lo + k * 16, 16), 16)
             total = tok[slot, rows, :].astype(F32)
             for other in others:
                 total = total + other[rows, :].astype(F32)
@@ -520,10 +530,10 @@
         slot = zs[dz] * 2 + yl
         pair[dz].wait_recv()
 
-        @pl.loop(0, YR // 48)
+        @pl.loop(0, YR // 32)
         def _(k):
-            rows = pl.ds(pl.multiple_of(ZR + k * 48, 16), 48)
-            some = pl.ds(pl.multiple_of(k * 48, 16), 48)
+            rows = pl.ds(pl.multiple_of(ZR + k * 32, 16), 32)
+            some = pl.ds(pl.multiple_of(k * 32, 16), 32)
             tok[slot, rows, :] = (
                 tok[slot, rows, :].astype(F32) + yb[dz, some, :].astype(F32)
             ).astype(BF)
@@ -617,7 +627,7 @@
             pltpu.SemaphoreType.DMA((COPIES,)),
         ],
         compiler_params=pltpu.CompilerParams(
-            collective_id=0, has_side_effects=True, vmem_limit_bytes=52 * 1024 * 1024
+            collective_id=0, has_side_effects=True, vmem_limit_bytes=60 * 1024 * 1024
         ),
         name="step",
     )(

time: 167 us -> 161 us (0.964)
  Pallas kernels: 161 us -> 158 us
  local copies, waits for them, and re-layouts: 4.92 us -> 2.74 us
    pallas_call x1, Pallas kernels: 161 us -> 158 us  [shards(): pl.pallas_call(kernel, out_shape=(jax.ShapeDtypeStruct((PR, F), BF), jax....]
    unnamed x12 -> x4, local copies, waits for them, and re-layouts: 4.92 us -> 2.74 us
where the time goes in v4:
time: 161 us
  Pallas kernels  158 us (98%)
  local copies, waits for them, and re-layouts  2.74 us (2%)
    pallas_call x1, Pallas kernels, shards(): pl.pallas_call(kernel, out_shape=(jax.ShapeDtypeStruct((PR, F), BF), jax....  158 us

profile of v4, /device:TPU:1, one launch (start us, length us, event | category | flops | bytes accessed | tf_op | source)
XLA Modules:
  0.0 161.2 jit_solution(3185878179671329304)
XLA Ops:
  0.6 157.8 %step.1 = (bf16[768,512]{1,0:T(8,128)(2,1)}, bf16[96,512]{1,0:T(8,128)(2,1)}) custom-call(bf16[768,512]{1,0:T(8,128)(2,1)} %bitcast.5, bf16[96,512]{1,0:T(8,128)(2,1)} %bitcast.7, s32[12,64]{1,0:T(8,128)} %mp_ref.1, s32[8,12]{1,0:T(8,128)} %bitcast.9, s32[12]{0:T(128)} %lab_ref.1, bf16[256,2048]{1,0:T(8,128)(2,1)} %hw_ref.1), custom_call_target="tpu_custom_call" | custom-call | tf_op jit(solution)/shard_map/step/pallas_call | solution.py:602
  158.5 0.0 copy-start
  158.5 2.1 %copy.10 = bf16[12,64,512]{2,1,0:T(8,128)(2,1)} copy(bf16[12,64,512]{2,1,0:T(8,128)(2,1)} %bitcast.6) | data formatting | bytes 1572864
  160.6 0.0 copy-done
  160.6 0.6 copy.11
Async XLA Ops:
  158.5 2.1 %copy-start = (bf16[96,512]{1,0:T(8,128)(2,1)S(1)}, bf16[96,512]{1,0:T(8,128)(2,1)}, u32[]{:S(2)}) copy-start(bf16[96,512]{1,0:T(8,128)(2,1)} %get-tuple-element.5) | copy-start | bytes 294916

commit v5 on v4

--- a/solution.py
+++ b/solution.py
@@ -211,6 +211,16 @@
         for copy in s[(dx, dy)]:
             copy.wait_recv()
 
+    def mm1_part(slot, half):
+        feats = pl.ds(pl.multiple_of(half * HD, HD), HD)
+
+        @pl.loop(0, 2)
+        def _(n):
+            cols = pl.ds(pl.multiple_of(n * (W // 2), W // 2), W // 2)
+            acc[:, cols] += jnp.dot(
+                tok[slot, :, feats], head[slot, feats, cols], preferred_element_type=F32
+            )
+
     def mm1(ready):
         @pl.loop(0, VOCAB)
         def _(slot):
@@ -229,61 +239,58 @@
     def near_hidden(slot):
         return slot % 2 == yl
 
+    def early(slot):
+        return near_hidden(slot) | (slot // 2 == z)
+
     def far_head(slot):
-        return jnp.logical_not(near_head(slot)) & (slot % 4 == xs[2])
+        return slot == yhs[1] * 4 + xs[2]
 
     def far_hidden(slot):
         return jnp.logical_not(near_hidden(slot)) & (slot // 2 == zs[2])
-
-    def far(slot):
-        return far_head(slot) | far_hidden(slot)
 
     for key in [("+", 1), ("-", 0), "f+", "f-"]:
         a[key].wait_recv()
     for dx in range(4):
         core_took(dx, 0)
-    mm1(lambda slot: near_head(slot) & near_hidden(slot))
+    mm1(lambda slot: near_head(slot) & early(slot))
     a[("o+", 0)].wait_recv()
     a_send("g+", hid(3, 1, 0), zdev[1])
     a[("o-", 1)].wait_recv()
     a_send("g-", hid(1, 1, 1), zdev[3])
     b[("o+", 0)].wait_recv()
     b_send("g+", 3, 1, ring[0], xdev[1])
+    to_core(3, 1, ring[0])
+    b_took(("r", 0), 0, 1, rest)
+    b_took(("o-", 0), 1, 1, (0, HY // 2))
+    core_took(0, 1)
+    mm1(lambda slot: (slot == yhs[1] * 4 + x) & early(slot))
     b[("o-", 1)].wait_recv()
     b_send("g-", 1, 1, ring[1], xdev[3])
-    to_core(3, 1, ring[0])
     to_core(1, 1, ring[1])
     a[("o+", 1)].wait_recv()
     a[("o-", 0)].wait_recv()
-    b_took(("r", 0), 0, 1, rest)
-    core_took(0, 1)
     mm1(
-        lambda slot: (
-            (near_head(slot) & jnp.logical_not(near_hidden(slot)))
-            | (slot == (1 - yh) * 4 + x)
-        )
+        lambda slot: (near_head(slot) | (slot == yhs[1] * 4 + x))
+        & jnp.logical_not(early(slot))
         & jnp.logical_not(far_hidden(slot))
     )
+    b_took(("r", 1), 1, 1, rest)
+    b_took(("o-", 2), 1, 1, (HY // 2, HY // 2))
     b_took(("o+", 1), 3, 1, ring[1])
-    b_took(("o-", 0), 1, 1, (0, HY // 2))
-    b_took(("o-", 2), 1, 1, (HY // 2, HY // 2))
-    b_took(("r", 1), 1, 1, rest)
     b_took(("r", 3), 3, 1, rest)
-    for dx in (1, 3):
-        core_took(dx, 1)
-    mm1(
-        lambda slot: jnp.logical_not(near_head(slot))
-        & (slot % 4 != x)
-        & jnp.logical_not(far(slot))
-    )
+    core_took(1, 1)
+    mm1(lambda slot: (slot == yhs[1] * 4 + xs[1]) & jnp.logical_not(far_hidden(slot)))
+    core_took(3, 1)
+    mm1(lambda slot: (slot == yhs[1] * 4 + xs[3]) & jnp.logical_not(far_hidden(slot)))
     b_took(("r", 2), 2, 1, rest)
     b_took("g+", 2, 1, ring[0])
     b_took("g-", 2, 1, ring[1])
     a["g+"].wait_recv()
     a["g-"].wait_recv()
     mm1(lambda slot: far_hidden(slot) & jnp.logical_not(far_head(slot)))
+    mm1_part(yhs[1] * 4 + xs[2], c)
     core_took(2, 1)
-    mm1(far_head)
+    mm1_part(yhs[1] * 4 + xs[2], 1 - c)
 
     def pool(base, length, weight, k, side, first):
         rows = pl.ds(pl.multiple_of(base + k * length, 8), length)

time: 161 us -> 157 us (0.975)
  Pallas kernels: 158 us -> 154 us
    pallas_call x1, Pallas kernels: 158 us -> 154 us  [shards(): pl.pallas_call(kernel, out_shape=(jax.ShapeDtypeStruct((PR, F), BF), jax....]
where the time goes in v5:
time: 157 us
  Pallas kernels  154 us (98%)
  local copies, waits for them, and re-layouts  2.74 us (2%)
    pallas_call x1, Pallas kernels, shards(): pl.pallas_call(kernel, out_shape=(jax.ShapeDtypeStruct((PR, F), BF), jax....  154 us

profile of v5, /device:TPU:1, one launch (start us, length us, event | category | flops | bytes accessed | tf_op | source)
XLA Modules:
  0.0 157.2 jit_solution(11521394110337371934)
XLA Ops:
  0.6 153.8 %step.1 = (bf16[768,512]{1,0:T(8,128)(2,1)}, bf16[96,512]{1,0:T(8,128)(2,1)}) custom-call(bf16[768,512]{1,0:T(8,128)(2,1)} %bitcast.5, bf16[96,512]{1,0:T(8,128)(2,1)} %bitcast.7, s32[12,64]{1,0:T(8,128)} %mp_ref.1, s32[8,12]{1,0:T(8,128)} %bitcast.9, s32[12]{0:T(128)} %lab_ref.1, bf16[256,2048]{1,0:T(8,128)(2,1)} %hw_ref.1), custom_call_target="tpu_custom_call" | custom-call | tf_op jit(solution)/shard_map/step/pallas_call | solution.py:609
  154.5 0.0 copy-start
  154.5 2.1 %copy.10 = bf16[12,64,512]{2,1,0:T(8,128)(2,1)} copy(bf16[12,64,512]{2,1,0:T(8,128)(2,1)} %bitcast.6) | data formatting | bytes 1572864
  156.6 0.0 copy-done
  156.6 0.6 copy.11
Async XLA Ops:
  154.5 2.1 %copy-start = (bf16[96,512]{1,0:T(8,128)(2,1)S(1)}, bf16[96,512]{1,0:T(8,128)(2,1)}, u32[]{:S(2)}) copy-start(bf16[96,512]{1,0:T(8,128)(2,1)} %get-tuple-element.5) | copy-start | bytes 294916

commit v6 on v5

--- a/solution.py
+++ b/solution.py
@@ -18,10 +18,10 @@
 QR = G * LQ
 R = PR + QR
 RH = R // 2
-ZR = 512
-ZH = ((0, 256), (256, 256))
+ZR = 464
+ZH = ((0, 240), (240, 224))
 YR = R - ZR
-YH = ((512, 176), (688, 176))
+YH = ((464, 208), (672, 192))
 F = 512
 W = 2048
 HD = 256
@@ -50,9 +50,9 @@
 def kernel(
     hp_ref,
     hq_ref,
-    mp_ref,
-    mq_ref,
-    lab_ref,
+    mp_hbm,
+    mq_hbm,
+    lab_hbm,
     hw_ref,
     gp_ref,
     gq_ref,
@@ -70,6 +70,9 @@
     rfull,
     ybuf,
     yb,
+    mp_ref,
+    mq_ref,
+    lab_ref,
     lsem,
     ssem,
     rsem,
@@ -93,6 +96,9 @@
         pltpu.make_async_copy(hp_ref, tok.at[v, pl.ds(0, PR)], lsem.at[0]),
         pltpu.make_async_copy(hq_ref, tok.at[v, pl.ds(PR, QR)], lsem.at[1]),
         pltpu.make_async_copy(hw_ref, head.at[own_head, pl.ds(c * HD, HD)], lsem.at[2]),
+        pltpu.make_async_copy(mp_hbm, mp_ref, lsem.at[3]),
+        pltpu.make_async_copy(mq_hbm, mq_ref, lsem.at[4]),
+        pltpu.make_async_copy(lab_hbm, lab_ref, lsem.at[5]),
     ]
     for copy in local:
         copy.start()
@@ -425,6 +431,80 @@
         )
         slopes[rows, :] = (acc[rows, :] * gain).astype(BF)
 
+    for copy in tok_sent:
+        copy.wait_send()
+
+    def part(dz, dy, lo, n):
+        return tok.at[zs[dz] * 2 + yls[dy], pl.ds(lo, n)]
+
+    def mm2(dz, dy):
+        slot = zs[dz] * 2 + yls[dy]
+
+        @pl.loop(0, F // 256)
+        def _(n):
+            cols = pl.ds(pl.multiple_of(n * 256, 256), 256)
+            tok[slot, :, cols] = lax.dot_general(
+                slopes[...],
+                head[slot, cols, :],
+                (((1,), (1,)), ((), ())),
+                preferred_element_type=F32,
+            ).astype(BF)
+
+    def mm2_pass(dz, dy):
+        slot = zs[dz] * 2 + yls[dy]
+
+        @pl.loop(0, F // 256)
+        def _(n):
+            cols = pl.ds(pl.multiple_of(n * 256, 256), 256)
+            tok[slot, pl.ds(0, PR), cols] = lax.dot_general(
+                slopes[pl.ds(0, PR), :],
+                head[slot, cols, :],
+                (((1,), (1,)), ((), ())),
+                preferred_element_type=F32,
+            ).astype(BF)
+
+    def mm2_rows(dz, dy, lo, n):
+        slot = zs[dz] * 2 + yls[dy]
+        rows = pl.ds(lo, n)
+        tok[slot, rows, :] = lax.dot_general(
+            slopes[rows, :],
+            head[slot],
+            (((1,), (1,)), ((), ())),
+            preferred_element_type=F32,
+        ).astype(BF)
+
+    def add_into(dz, dy, lo, size, *others):
+        slot = zs[dz] * 2 + yls[dy]
+
+        @pl.loop(0, size // 16)
+        def _(k):
+            rows = pl.ds(pl.multiple_of(lo + k * 16, 16), 16)
+            total = tok[slot, rows, :].astype(F32)
+            for other in others:
+                total = total + other[rows, :].astype(F32)
+            tok[slot, rows, :] = total.astype(BF)
+
+    def out(src, dst, dev):
+        copy = remote(src, dst, dev)
+        sent.append(copy)
+        return copy
+
+    def to_ring(dz, dy, lo, n, ref):
+        dev = zdev[1] if ref == 0 else zdev[3]
+        return out(part(dz, dy, lo, n), rfull.at[dy, ref, pl.ds(lo, n)], dev)
+
+    def to_half(dy, lo, n, ref):
+        dev = zdev[1] if ref == 0 else zdev[3]
+        return out(part(2, dy, lo, n), rhalf.at[dy, ref, pl.ds(lo, n)], dev)
+
+    def to_pair(dz, lo, n):
+        return out(part(dz, 1, lo, n), yb.at[dz, pl.ds(lo - ZR, n)], yldev)
+
+    pair = {0: [], 1: [], 2: [], 3: []}
+    for dz in (2, 1):
+        mm2_rows(dz, 1, PR, QR)
+        pair[dz].append(to_pair(dz, PR, QR))
+
     spread_q[7].wait_recv()
     for copy in handed_q:
         copy.wait_recv()
@@ -453,62 +533,6 @@
             rows = pl.ds(pl.multiple_of(k * 16, 16), 16)
             slopes[rows, :] = (acc[rows, :] * factor[0, pl.ds(k // (LP // 16), 1), :]).astype(BF)
 
-    for copy in tok_sent:
-        copy.wait_send()
-
-    def part(dz, dy, lo, n):
-        return tok.at[zs[dz] * 2 + yls[dy], pl.ds(lo, n)]
-
-    def mm2(dz, dy):
-        slot = zs[dz] * 2 + yls[dy]
-
-        @pl.loop(0, F // 256)
-        def _(n):
-            cols = pl.ds(pl.multiple_of(n * 256, 256), 256)
-            tok[slot, :, cols] = lax.dot_general(
-                slopes[...],
-                head[slot, cols, :],
-                (((1,), (1,)), ((), ())),
-                preferred_element_type=F32,
-            ).astype(BF)
-
-    def mm2_rows(dz, dy, lo, n):
-        slot = zs[dz] * 2 + yls[dy]
-        rows = pl.ds(lo, n)
-        tok[slot, rows, :] = lax.dot_general(
-            slopes[rows, :],
-            head[slot],
-            (((1,), (1,)), ((), ())),
-            preferred_element_type=F32,
-        ).astype(BF)
-
-    def add_into(dz, dy, lo, size, *others):
-        slot = zs[dz] * 2 + yls[dy]
-
-        @pl.loop(0, size // 16)
-        def _(k):
-            rows = pl.ds(pl.multiple_of(lo + k * 16, 16), 16)
-            total = tok[slot, rows, :].astype(F32)
-            for other in others:
-                total = total + other[rows, :].astype(F32)
-            tok[slot, rows, :] = total.astype(BF)
-
-    def out(src, dst, dev):
-        copy = remote(src, dst, dev)
-        sent.append(copy)
-        return copy
-
-    def to_ring(dz, dy, lo, n, ref):
-        dev = zdev[1] if ref == 0 else zdev[3]
-        return out(part(dz, dy, lo, n), rfull.at[dy, ref, pl.ds(lo, n)], dev)
-
-    def to_half(dy, lo, n, ref):
-        dev = zdev[1] if ref == 0 else zdev[3]
-        return out(part(2, dy, lo, n), rhalf.at[dy, ref, pl.ds(lo, n)], dev)
-
-    def to_pair(dz):
-        return out(part(dz, 1, ZR, YR), yb.at[dz], yldev)
-
     pass_slopes(*ZH[0])
     mm2_rows(2, 1, *ZH[0])
     up = to_half(1, *ZH[0], 0)
@@ -516,14 +540,14 @@
     mm2_rows(2, 1, *ZH[1])
     down = to_half(1, *ZH[1], 1)
     pass_slopes(ZR, PR - ZR)
-    mm2_rows(2, 1, ZR, YR)
-    pair = {2: to_pair(2)}
-    mm2(1, 1)
+    mm2_rows(2, 1, ZR, PR - ZR)
+    pair[2].append(to_pair(2, ZR, PR - ZR))
+    mm2_pass(1, 1)
     other_plane = [to_ring(1, 1, *ZH[1], 0)]
-    pair[1] = to_pair(1)
+    pair[1].append(to_pair(1, ZR, PR - ZR))
     mm2(3, 1)
     other_plane.append(to_ring(3, 1, *ZH[0], 1))
-    pair[3] = to_pair(3)
+    pair[3].append(to_pair(3, ZR, YR))
     up.wait_recv()
     add_into(1, 1, *ZH[0], rhalf.at[1, 0])
     other_plane.append(to_ring(1, 1, *ZH[0], 0))
@@ -535,12 +559,13 @@
 
     def add_pair(dz):
         slot = zs[dz] * 2 + yl
-        pair[dz].wait_recv()
-
-        @pl.loop(0, YR // 32)
+        for copy in pair[dz]:
+            copy.wait_recv()
+
+        @pl.loop(0, YR // 16)
         def _(k):
-            rows = pl.ds(pl.multiple_of(ZR + k * 32, 16), 32)
-            some = pl.ds(pl.multiple_of(k * 32, 16), 32)
+            rows = pl.ds(pl.multiple_of(ZR + k * 16, 16), 16)
+            some = pl.ds(pl.multiple_of(k * 16, 16), 16)
             tok[slot, rows, :] = (
                 tok[slot, rows, :].astype(F32) + yb[dz, some, :].astype(F32)
             ).astype(BF)
@@ -603,16 +628,15 @@
 
 
 def shards(hidden_pass, hidden_query, mask_pass, mask_query, labels, head_weight):
-    anywhere = pl.BlockSpec(memory_space=pl.ANY)
+    hbm = pl.BlockSpec(memory_space=pltpu.HBM)
     vmem = pl.BlockSpec(memory_space=pltpu.VMEM)
-    smem = pl.BlockSpec(memory_space=pltpu.SMEM)
     grad_pass, grad_query = pl.pallas_call(
         kernel,
         out_shape=(
             jax.ShapeDtypeStruct((PR, F), BF),
             jax.ShapeDtypeStruct((QR, F), BF),
         ),
-        in_specs=[anywhere, anywhere, vmem, vmem, smem, anywhere],
+        in_specs=[hbm] * 6,
         out_specs=(vmem, vmem),
         scratch_shapes=[
             pltpu.VMEM((VOCAB, R, F), BF),
@@ -629,21 +653,29 @@
             pltpu.VMEM((2, 2, R, F), BF),
             pltpu.VMEM((R, F), BF),
             pltpu.VMEM((4, YR, F), BF),
-            pltpu.SemaphoreType.DMA((3,)),
+            pltpu.VMEM((G, LP), jnp.int32),
+            pltpu.VMEM((LQ, G), jnp.int32),
+            pltpu.SMEM((G,), jnp.int32),
+            pltpu.SemaphoreType.DMA((6,)),
             pltpu.SemaphoreType.DMA((COPIES,)),
             pltpu.SemaphoreType.DMA((COPIES,)),
         ],
         compiler_params=pltpu.CompilerParams(
-            collective_id=0, has_side_effects=True, vmem_limit_bytes=60 * 1024 * 1024
+            collective_id=0, has_side_effects=True, vmem_limit_bytes=52 * 1024 * 1024
         ),
         name="step",
     )(
-        hidden_pass.reshape(PR, F),
-        hidden_query.reshape(QR, F),
-        mask_pass,
-        mask_query.T,
-        labels,
-        head_weight,
+        *(
+            pltpu.with_memory_space_constraint(x, pltpu.HBM)
+            for x in (
+                hidden_pass.reshape(PR, F),
+                hidden_query.reshape(QR, F),
+                mask_pass,
+                mask_query.T,
+                labels,
+                head_weight,
+            )
+        )
     )
     return (
         grad_pass.reshape(G, LP, F),

time: 157 us -> 153 us (0.975)
  Pallas kernels: 154 us -> 150 us
    pallas_call x1, Pallas kernels: 154 us -> 150 us  [shards(): pl.pallas_call(kernel, out_shape=(jax.ShapeDtypeStruct((PR, F), BF), jax....]
where the time goes in v6:
time: 153 us
  Pallas kernels  150 us (98%)
    pallas_call x1, Pallas kernels, shards(): pl.pallas_call(kernel, out_shape=(jax.ShapeDtypeStruct((PR, F), BF), jax....  150 us

profile of v6, /device:TPU:1, one launch (start us, length us, event | category | flops | bytes accessed | tf_op | source)
XLA Modules:
  0.0 152.7 jit_solution(14397081294868612184)
XLA Ops:
  0.6 150.5 %step.1 = (bf16[768,512]{1,0:T(8,128)(2,1)S(1)}, bf16[96,512]{1,0:T(8,128)(2,1)S(1)}) custom-call(bf16[768,512]{1,0:T(8,128)(2,1)} %bitcast.7, bf16[96,512]{1,0:T(8,128)(2,1)} %bitcast.8, s32[12,64]{1,0:T(8,128)} %mp_hbm.1, s32[8,12]{1,0:T(8,128)} %bitcast.9, s32[12]{0:T(128)} %lab_hbm.1, bf16[256,2048]{1,0:T(8,128)(2,1)} %hw_ref.1), custom_call_target="tpu_custom_call" | custom-call | tf_op jit(solution)/shard_map/step/pallas_call | solution.py:633
  151.1 0.9 copy.10
  152.0 0.6 copy.11

commit v7 on v6

--- a/solution.py
+++ b/solution.py
@@ -18,16 +18,17 @@
 QR = G * LQ
 R = PR + QR
 RH = R // 2
-ZR = 464
-ZH = ((0, 240), (240, 224))
+ZR = 448
+ZH = ((0, 256), (256, 192))
 YR = R - ZR
-YH = ((464, 208), (672, 192))
+YH = ((448, 208), (656, 208))
 F = 512
 W = 2048
 HD = 256
 HH = HD // 2
 HY = 96
 HX = HD - 2 * HY
+LANES = 256
 PAD = 16
 ROWS = 16
 VOCAB = 8
@@ -73,6 +74,7 @@
     mp_ref,
     mq_ref,
     lab_ref,
+    mask,
     lsem,
     ssem,
     rsem,
@@ -178,6 +180,17 @@
 
     acc[...] = jnp.zeros_like(acc)
     totals[...] = jnp.zeros_like(totals)
+
+    @pl.loop(0, G)
+    def _(k):
+        line = mp_ref[pl.ds(k, 1), :].astype(F32)
+        shape = (LP, LP)
+        eye = lax.broadcasted_iota(jnp.int32, shape, 0) == lax.broadcasted_iota(jnp.int32, shape, 1)
+        column = jnp.sum(jnp.where(eye, jnp.broadcast_to(line, shape), 0.0), axis=1, keepdims=True)
+        mask[pl.ds(pl.multiple_of(k * LP, LP), LP), :] = jnp.broadcast_to(column, (LP, LANES))
+        here = lax.broadcasted_iota(jnp.int32, (LQ, G), 1) == k
+        column = jnp.sum(jnp.where(here, mq_ref[...].astype(F32), 0.0), axis=1, keepdims=True)
+        mask[pl.ds(pl.multiple_of(PR + k * LQ, LQ), LQ), :] = jnp.broadcast_to(column, (LQ, LANES))
 
     a[("+", 0)].wait_recv()
     a_send("f+", hid(3, 0, 0), zdev[1])
@@ -298,35 +311,25 @@
     core_took(2, 1)
     mm1_part(yhs[1] * 4 + xs[2], 1 - c)
 
-    def pool(base, length, weight, k, side, first):
+    def pool(base, length, k, side, first):
         rows = pl.ds(pl.multiple_of(base + k * length, 8), length)
-        for n in range(first, first + W // 2, 256):
-            cols = pl.ds(n, 256)
-            high = jnp.maximum(acc[rows, cols], 0.0)
-            act = jnp.log1p(high)
+        weight = mask[rows, :]
+        for n in range(first, first + W // 2, LANES):
+            cols = pl.ds(n, LANES)
+            act = jnp.log1p(jnp.maximum(acc[rows, cols], 0.0))
             square = act * act
             totals[side, pl.ds(k, 1), cols] = jnp.sum(
                 square * square * weight, axis=0, keepdims=True
             )
 
-    def slope(base, length, weight, k):
+    def slope(base, length, k):
         rows = pl.ds(pl.multiple_of(base + k * length, 8), length)
-        for n in range(0, W, 256):
-            cols = pl.ds(n, 256)
+        weight = mask[rows, :]
+        for n in range(0, W, LANES):
+            cols = pl.ds(n, LANES)
             high = jnp.maximum(acc[rows, cols], 0.0)
             act = jnp.log1p(high)
             acc[rows, cols] = weight * (act * act * act) / (1.0 + high)
-
-    def line_weight(k):
-        line = mp_ref[pl.ds(k, 1), :].astype(F32)
-        shape = (LP, LP)
-        eye = lax.broadcasted_iota(jnp.int32, shape, 0) == lax.broadcasted_iota(jnp.int32, shape, 1)
-        return jnp.sum(jnp.where(eye, jnp.broadcast_to(line, shape), 0.0), axis=1, keepdims=True)
-
-    def query_weight(k):
-        shape = (LQ, G)
-        here = lax.broadcasted_iota(jnp.int32, shape, 1) == k
-        return jnp.sum(jnp.where(here, mq_ref[...].astype(F32), 0.0), axis=1, keepdims=True)
 
     def fourth_root(t):
         return jnp.sqrt(jnp.sqrt(t))
@@ -351,24 +354,25 @@
 
         @pl.loop(0, G)
         def _(k):
-            pool(0, LP, line_weight(k), k, 0, first)
+            pool(0, LP, k, 0, first)
 
         allp[r, :, cols] = (fourth_root(totals[0, :, cols] + 1.0) - 1.0).astype(BF)
         spread_p.append((cols, spread(allp, cols)))
 
     @pl.loop(0, G)
     def _(k):
-        pool(PR, LQ, query_weight(k), k, 1, 0)
-        pool(PR, LQ, query_weight(k), k, 1, W // 2)
+        pool(PR, LQ, k, 1, 0)
+        pool(PR, LQ, k, 1, W // 2)
 
     whole = pl.ds(0, W)
     allq[r] = (fourth_root(totals[1] + 1.0) - 1.0).astype(BF)
 
+    spread_q = spread(allq, whole)
+
     @pl.loop(0, G)
     def _(k):
-        slope(0, LP, line_weight(k), k)
-
-    spread_q = spread(allq, whole)
+        slope(0, LP, k)
+
     handed_p = []
     for cols, copies in spread_p:
         handed_p += hand_on(allp, cols, copies)
@@ -384,7 +388,7 @@
 
     @pl.loop(0, G)
     def _(k):
-        slope(PR, LQ, query_weight(k), k)
+        slope(PR, LQ, k)
 
     row_at = lax.broadcasted_iota(jnp.int32, (PAD, ROWS * PAD), 0)
     col_at = lax.broadcasted_iota(jnp.int32, (PAD, ROWS * PAD), 1)
@@ -505,17 +509,18 @@
         mm2_rows(dz, 1, PR, QR)
         pair[dz].append(to_pair(dz, PR, QR))
 
-    spread_q[7].wait_recv()
-    for copy in handed_q:
-        copy.wait_recv()
-    for copy in group:
-        copy.wait_recv()
+    factor[0] = tail(totals[0] + 1.0)
     pick = jnp.where(
         lax.broadcasted_iota(jnp.int32, (ROWS * PAD, PAD), 0)
         == r * PAD + lax.broadcasted_iota(jnp.int32, (ROWS * PAD, PAD), 1),
         1.0,
         0.0,
     ).astype(BF)
+    spread_q[7].wait_recv()
+    for copy in handed_q:
+        copy.wait_recv()
+    for copy in group:
+        copy.wait_recv()
     mine = jnp.dot(
         gbuf[...].reshape(ROWS * PAD, ROWS * PAD), pick, preferred_element_type=F32
     ).astype(BF)
@@ -525,13 +530,15 @@
         (((0,), (0,)), ((), ())),
         preferred_element_type=F32,
     )
-    factor[0] = pass_grad * tail(totals[0] + 1.0)
+    factor[0] = pass_grad * factor[0]
 
     def pass_slopes(lo, n):
-        @pl.loop(lo // 16, (lo + n) // 16)
+        @pl.loop(lo // LP, (lo + n) // LP)
         def _(k):
-            rows = pl.ds(pl.multiple_of(k * 16, 16), 16)
-            slopes[rows, :] = (acc[rows, :] * factor[0, pl.ds(k // (LP // 16), 1), :]).astype(BF)
+            rows = pl.ds(pl.multiple_of(k * LP, LP), LP)
+            for m in range(0, W, 512):
+                cols = pl.ds(m, 512)
+                slopes[rows, cols] = (acc[rows, cols] * factor[0, pl.ds(k, 1), cols]).astype(BF)
 
     pass_slopes(*ZH[0])
     mm2_rows(2, 1, *ZH[0])
@@ -555,7 +562,8 @@
     add_into(3, 1, *ZH[1], rhalf.at[1, 1])
     other_plane.append(to_ring(3, 1, *ZH[1], 1))
     mm2(0, 1)
-    last = [out(part(0, 1, ZR, YR), ybuf.at[pl.ds(ZR, YR)], yldev)]
+    last_z = []
+    last_y = [out(part(0, 1, ZR, YR), ybuf.at[pl.ds(ZR, YR)], yldev)]
 
     def add_pair(dz):
         slot = zs[dz] * 2 + yl
@@ -577,33 +585,30 @@
     up_y = to_half(0, *YH[0], 0)
     down_y = to_half(0, *YH[1], 1)
     mm2(1, 0)
-    last.append(to_ring(1, 0, *ZH[1], 0))
+    last_z.append(to_ring(1, 0, *ZH[1], 0))
     mm2(3, 0)
-    last.append(to_ring(3, 0, *ZH[0], 1))
+    last_z.append(to_ring(3, 0, *ZH[0], 1))
     for copy in other_plane:
         copy.wait_recv()
     add_into(0, 1, 0, ZR, rfull.at[1, 0], rfull.at[1, 1])
-    last.append(out(part(0, 1, 0, ZR), ybuf.at[pl.ds(0, ZR)], yldev))
+    last_z.append(out(part(0, 1, 0, ZR), ybuf.at[pl.ds(0, ZR)], yldev))
     up.wait_recv()
     add_into(1, 0, *ZH[0], rhalf.at[0, 0])
-    last.append(to_ring(1, 0, *ZH[0], 0))
+    last_z.append(to_ring(1, 0, *ZH[0], 0))
     down.wait_recv()
     add_into(3, 0, *ZH[1], rhalf.at[0, 1])
-    last.append(to_ring(3, 0, *ZH[1], 1))
+    last_z.append(to_ring(3, 0, *ZH[1], 1))
     add_pair(1)
-    last.append(to_ring(1, 0, *YH[1], 0))
+    last_y.append(to_ring(1, 0, *YH[1], 0))
     add_pair(3)
-    last.append(to_ring(3, 0, *YH[0], 1))
+    last_y.append(to_ring(3, 0, *YH[0], 1))
     mm2(0, 0)
     up_y.wait_recv()
     add_into(1, 0, *YH[0], rhalf.at[0, 0])
-    last.append(to_ring(1, 0, *YH[0], 0))
+    last_y.append(to_ring(1, 0, *YH[0], 0))
     down_y.wait_recv()
     add_into(3, 0, *YH[1], rhalf.at[0, 1])
-    last.append(to_ring(3, 0, *YH[1], 1))
-    for copy in last:
-        copy.wait_recv()
-
+    last_y.append(to_ring(3, 0, *YH[1], 1))
     def total(rows):
         return (
             tok[v, rows, :].astype(F32)
@@ -612,11 +617,18 @@
             + ybuf[rows, :].astype(F32)
         ).astype(BF)
 
-    @pl.loop(0, PR // 48)
-    def _(k):
-        rows = pl.ds(pl.multiple_of(k * 48, 16), 48)
-        gp_ref[rows, :] = total(rows)
-
+    def finish(lo, n):
+        @pl.loop(0, n // 64)
+        def _(k):
+            rows = pl.ds(pl.multiple_of(lo + k * 64, 16), 64)
+            gp_ref[rows, :] = total(rows)
+
+    for copy in last_z:
+        copy.wait_recv()
+    finish(0, ZR)
+    for copy in last_y:
+        copy.wait_recv()
+    finish(ZR, PR - ZR)
     for k in range(QR // 48):
         gq_ref[pl.ds(k * 48, 48), :] = total(pl.ds(PR + k * 48, 48))
 
@@ -656,6 +668,7 @@
             pltpu.VMEM((G, LP), jnp.int32),
             pltpu.VMEM((LQ, G), jnp.int32),
             pltpu.SMEM((G,), jnp.int32),
+            pltpu.VMEM((R, LANES), F32),
             pltpu.SemaphoreType.DMA((6,)),
             pltpu.SemaphoreType.DMA((COPIES,)),
             pltpu.SemaphoreType.DMA((COPIES,)),

time: 153 us -> 151 us (0.987)
    pallas_call x1, Pallas kernels: 150 us -> 149 us  [shards(): pl.pallas_call(kernel, out_shape=(jax.ShapeDtypeStruct((PR, F), BF), jax....]
where the time goes in v7:
time: 151 us
  Pallas kernels  149 us (99%)
  local copies, waits for them, and re-layouts  1.52 us (1%)
    pallas_call x1, Pallas kernels, shards(): pl.pallas_call(kernel, out_shape=(jax.ShapeDtypeStruct((PR, F), BF), jax....  149 us

profile of v7, /device:TPU:1, one launch (start us, length us, event | category | flops | bytes accessed | tf_op | source)
XLA Modules:
  0.0 151.0 jit_solution(16661333800568882384)
XLA Ops:
  0.6 148.9 %step.1 = (bf16[768,512]{1,0:T(8,128)(2,1)S(1)}, bf16[96,512]{1,0:T(8,128)(2,1)S(1)}) custom-call(bf16[768,512]{1,0:T(8,128)(2,1)} %bitcast.7, bf16[96,512]{1,0:T(8,128)(2,1)} %bitcast.8, s32[12,64]{1,0:T(8,128)} %mp_hbm.1, s32[8,12]{1,0:T(8,128)} %bitcast.9, s32[12]{0:T(128)} %lab_hbm.1, bf16[256,2048]{1,0:T(8,128)(2,1)} %hw_ref.1), custom_call_target="tpu_custom_call" | custom-call | tf_op jit(solution)/shard_map/step/pallas_call | solution.py:645
  149.5 0.9 copy.10
  150.4 0.6 copy.11

commit v8 on v7

--- a/solution.py
+++ b/solution.py
@@ -480,9 +480,11 @@
     def add_into(dz, dy, lo, size, *others):
         slot = zs[dz] * 2 + yls[dy]
 
-        @pl.loop(0, size // 16)
+        block = 64 if size % 64 == 0 else 16
+
+        @pl.loop(0, size // block)
         def _(k):
-            rows = pl.ds(pl.multiple_of(lo + k * 16, 16), 16)
+            rows = pl.ds(pl.multiple_of(lo + k * block, 16), block)
             total = tok[slot, rows, :].astype(F32)
             for other in others:
                 total = total + other[rows, :].astype(F32)

time: 151 us -> 151 us (level)
  no operation moved by 1% of the time
where the time goes in v8:
time: 151 us
  Pallas kernels  149 us (99%)
  local copies, waits for them, and re-layouts  1.52 us (1%)
    pallas_call x1, Pallas kernels, shards(): pl.pallas_call(kernel, out_shape=(jax.ShapeDtypeStruct((PR, F), BF), jax....  149 us

profile of v8, /device:TPU:1, one launch (start us, length us, event | category | flops | bytes accessed | tf_op | source)
XLA Modules:
  0.0 151.0 jit_solution(13072769714551887369)
XLA Ops:
  0.6 148.9 %step.1 = (bf16[768,512]{1,0:T(8,128)(2,1)S(1)}, bf16[96,512]{1,0:T(8,128)(2,1)S(1)}) custom-call(bf16[768,512]{1,0:T(8,128)(2,1)} %bitcast.7, bf16[96,512]{1,0:T(8,128)(2,1)} %bitcast.8, s32[12,64]{1,0:T(8,128)} %mp_hbm.1, s32[8,12]{1,0:T(8,128)} %bitcast.9, s32[12]{0:T(128)} %lab_hbm.1, bf16[256,2048]{1,0:T(8,128)(2,1)} %hw_ref.1), custom_call_target="tpu_custom_call" | custom-call | tf_op jit(solution)/shard_map/step/pallas_call | solution.py:647
  149.5 0.9 copy.10
  150.4 0.6 copy.11
